TPU v7x, 32 devices: a whole 2x2x4 slice. The times are simulated.
32 devices in a mesh: groups: 2 (over y), role: 4 (over x, core), tp: 4 (over z).
Axes of the slice: x: 2, y: 2, z: 4, core: 2. Of those that a mesh axis runs over, the one named last changes fastest.
Arguments:
- residual: bfloat16 [64, 8192], P(('groups', 'tp'), 'role'), parts along dimension 0, may hold values from -20 to 20
- attn_gain: float32 [8192], P('role'), may hold values from 0.1 to 1.9
- w_query: bfloat16 [8192, 4096], P('role', 'tp'), may hold values from -0.0625 to 0.0625
- w_key: bfloat16 [8192, 512], P('role', 'tp'), may hold values from -0.0625 to 0.0625
- w_value: bfloat16 [8192, 512], P('role', 'tp'), may hold values from -0.0625 to 0.0625
- w_output: bfloat16 [4096, 8192], P('tp', 'role'), may hold values from -0.09375 to 0.09375
- cache_keys: bfloat16 [64, 256, 512], P(('groups', 'role', 'tp')), parts along dimension 0, may hold values from -300 to 300
- cache_values: bfloat16 [64, 256, 512], P(('groups', 'role', 'tp')), parts along dimension 0, may hold values from -12 to 12
- lengths: int32 [64], P(('groups', 'role', 'tp')), parts along dimension 0, may hold values from 2 to 256
- served: int32 [64], P('groups'), parts along dimension 0, may hold values 0 or 1
- ffn_gain: float32 [8192], P('role'), may hold values from 0.1 to 1.9
- w_gate: bfloat16 [8192, 14336], P('role', 'tp'), may hold values from -0.0625 to 0.0625
- w_up: bfloat16 [8192, 14336], P('role', 'tp'), may hold values from -0.0625 to 0.0625
- w_down: bfloat16 [14336, 8192], P('tp', 'role'), may hold values from -0.046875 to 0.046875
Outputs:
- layer_out: bfloat16 [64, 8192], P(('groups', 'tp'), 'role'), parts along dimension 0
There are 2 independent parts, one for each index of `groups`. A program takes and returns all parts, laid end to end along the dimension named above; an argument that names none is the same for every part. Nothing has to cross between parts.
Inputs may be any that keep to these rules, and one draw needn't show every extreme that they name: Each request's new token stands at position lengths; cached positions from lengths on are unused.
All inputs are finite; a program needn't handle non-finite values.
Results may differ from a plain program's by a relative error of at most 0.024.
Values may be sent and summed in bfloat16 or wider, within the bound.
No kernel may reach another device: no remote copies, remote signals or barrier semaphores. Data moves between devices by JAX's collectives and lax.ppermute only.
A program may use at most 128 MiB of HBM per device.

v0:
```python
import functools
import math

import jax
import jax.numpy as jnp
from jax import lax
from jax.experimental import pallas as pl
from jax.experimental.pallas import tpu as pltpu
from jax.sharding import PartitionSpec as P


D = 8192
HEADS = 32
KV_HEADS = 4
HEAD_DIM = 128
WINDOW = 256
GROUP = 8


epsilon = 1e-05
rope_base = 500000.0


def rotate(vectors, positions):
    halfway = vectors.shape[-1] // 2
    frequency = jnp.power(
        jnp.float32(rope_base), -jnp.arange(halfway, dtype=jnp.float32) * 2.0 / vectors.shape[-1]
    )
    angles = positions.astype(jnp.float32)[:, None, None] * frequency[None, None, :]
    cosine = jnp.cos(angles)
    sine_part = jnp.sin(angles)
    leading = vectors[..., :halfway]
    trailing = vectors[..., halfway:]
    return jnp.concatenate(
        [leading * cosine - trailing * sine_part, trailing * cosine + leading * sine_part], axis=-1
    )


def attend(queries, new_key, new_value, keys, values, lengths):
    batch_rows = queries.shape[0]
    factor = HEAD_DIM ** (-0.5)
    grouped = queries.reshape(batch_rows, KV_HEADS, GROUP, HEAD_DIM)
    key_blocks = keys.reshape(batch_rows, WINDOW, KV_HEADS, HEAD_DIM)
    value_blocks = values.reshape(batch_rows, WINDOW, KV_HEADS, HEAD_DIM)
    scores = (
        jnp.einsum("nkgd,nwkd->nkgw", grouped, key_blocks, preferred_element_type=jnp.float32)
        * factor
    )
    self_score = (
        jnp.einsum("nkgd,nkd->nkg", grouped, new_key, preferred_element_type=jnp.float32) * factor
    )
    usable = jnp.arange(WINDOW, dtype=jnp.int32)[None, :] < lengths[:, None]
    scores = jnp.where(usable[:, None, None, :], scores, -jnp.inf)
    highest = jnp.maximum(jnp.max(scores, axis=-1), self_score)
    weights = jnp.exp(scores - highest[..., None])
    self_weight = jnp.exp(self_score - highest)
    denominator = jnp.sum(weights, axis=-1) + self_weight
    chances = (weights / denominator[..., None]).astype(jnp.bfloat16)
    self_chance = (self_weight / denominator).astype(jnp.bfloat16)
    attended = jnp.einsum(
        "nkgw,nwkd->nkgd", chances, value_blocks, preferred_element_type=jnp.float32
    )
    attended = (
        attended
        + self_chance.astype(jnp.float32)[..., None] * new_value.astype(jnp.float32)[:, :, None, :]
    )
    return attended.reshape(batch_rows, HEADS * HEAD_DIM).astype(jnp.bfloat16)


def feed_forward(middle, ffn_gain, w_gate, w_up, w_down):
    widened = middle.astype(jnp.float32)
    squares = lax.psum(jnp.sum(widened * widened, axis=1), "role")
    inverse = lax.rsqrt(squares / D + epsilon)
    mid_normed = (widened * inverse[:, None] * ffn_gain[None, :]).astype(jnp.bfloat16)
    gate_part = jnp.dot(mid_normed, w_gate, preferred_element_type=jnp.float32)
    up_part = jnp.dot(mid_normed, w_up, preferred_element_type=jnp.float32)
    gate_total, up_total = (
        lax.psum(gate_part.astype(jnp.bfloat16), "role").astype(jnp.float32),
        lax.psum(up_part.astype(jnp.bfloat16), "role").astype(jnp.float32),
    )
    hidden = (jax.nn.silu(gate_total) * up_total).astype(jnp.bfloat16)
    down_terms = jnp.dot(hidden, w_down, preferred_element_type=jnp.float32)
    return lax.psum_scatter(
        down_terms.astype(jnp.bfloat16), "tp", scatter_dimension=0, tiled=True
    ).astype(jnp.float32)


def local(
    residual,
    attn_gain,
    w_query,
    w_key,
    w_value,
    w_output,
    cache_keys,
    cache_values,
    lengths,
    served,
    ffn_gain,
    w_gate,
    w_up,
    w_down,
):
    own_rows = residual.shape[0]
    tp_count = lax.axis_size("tp")
    row_start = lax.axis_index("tp") * own_rows
    live_own = lax.dynamic_slice_in_dim(served, row_start, own_rows, 0).astype(jnp.float32)[:, None]
    rows_all = lax.all_gather(residual, "tp", axis=0, tiled=True)
    widened = rows_all.astype(jnp.float32)
    squares = lax.psum(jnp.sum(widened * widened, axis=1), "role")
    inverse = lax.rsqrt(squares / D + epsilon)
    normed = (widened * inverse[:, None] * attn_gain[None, :]).astype(jnp.bfloat16)
    partial_value = jnp.concatenate(
        [
            jnp.dot(normed, w_query, preferred_element_type=jnp.float32),
            jnp.dot(normed, w_key, preferred_element_type=jnp.float32),
            jnp.dot(normed, w_value, preferred_element_type=jnp.float32),
        ],
        axis=1,
    )
    summed = lax.psum_scatter(
        partial_value.astype(jnp.bfloat16), "role", scatter_dimension=0, tiled=True
    ).astype(jnp.float32)
    gathered = lax.all_to_all(
        summed.astype(jnp.bfloat16), "tp", split_axis=0, concat_axis=1, tiled=True
    ).astype(summed.dtype)
    local_rows = gathered.shape[0]
    query_cols = w_query.shape[1]
    kv_cols = w_key.shape[1]
    blocks = gathered.reshape(local_rows, tp_count, query_cols + 2 * kv_cols)
    queries = blocks[:, :, :query_cols].reshape(local_rows, HEADS, HEAD_DIM)
    new_key = blocks[:, :, query_cols : query_cols + kv_cols].reshape(
        local_rows, KV_HEADS, HEAD_DIM
    )
    new_value = (
        blocks[:, :, query_cols + kv_cols :]
        .reshape(local_rows, KV_HEADS, HEAD_DIM)
        .astype(jnp.bfloat16)
    )
    queries = rotate(queries, lengths).astype(jnp.bfloat16)
    new_key = rotate(new_key, lengths).astype(jnp.bfloat16)
    attended = attend(queries, new_key, new_value, cache_keys, cache_values, lengths)
    head_block = lax.all_to_all(attended, "tp", split_axis=1, concat_axis=0, tiled=True)
    attn_terms = jnp.dot(
        lax.all_gather(head_block, "role", axis=0, tiled=True),
        w_output,
        preferred_element_type=jnp.float32,
    )
    attn = lax.psum_scatter(
        attn_terms.astype(jnp.bfloat16), "tp", scatter_dimension=0, tiled=True
    ).astype(jnp.float32)
    middle_own = (residual.astype(jnp.float32) + live_own * attn).astype(jnp.bfloat16)
    middle = lax.all_gather(middle_own, "tp", axis=0, tiled=True)
    ffn = feed_forward(middle, ffn_gain, w_gate, w_up, w_down)
    return (middle_own.astype(jnp.float32) + live_own * ffn).astype(jnp.bfloat16)


LANES = 128
MIB = 2**20
COVER = (100, 1, 1, 1, 10, 10, 10, 1, 1, 1)
CHUNK = 512
FIRST_PART = 57


def exchange_fits(residual, w_query, w_key, w_gate):
    tp_count, role_count = lax.axis_size("tp"), lax.axis_size("role")
    return (
        tp_count == KV_HEADS
        and role_count == 4
        and residual.shape[0] % 8 == 0
        and residual.shape[1] % (2 * LANES) == 0
        and w_query.shape[1] == GROUP * LANES
        and w_key.shape[1] == LANES
        and w_gate.shape[1] % (4 * LANES) == 0
        and w_gate.shape[1] >= 8 * LANES
    )


def swap(value, axis, distance):
    count = lax.axis_size(axis)
    return lax.ppermute(value, axis, [(i, i ^ distance) for i in range(count)])


def in_vmem(value):
    return pltpu.with_memory_space_constraint(value, pltpu.VMEM)


def call(kernel, outs, args, scratch=(), limit=4 * MIB, smem=0, cost=0):
    specs = [pl.BlockSpec(memory_space=pltpu.SMEM)] * smem
    specs += [pl.BlockSpec(memory_space=pltpu.VMEM)] * (len(args) - smem)
    return pl.pallas_call(
        kernel,
        out_shape=outs,
        in_specs=specs,
        out_specs=[pl.BlockSpec(memory_space=pltpu.VMEM)] * len(outs),
        scratch_shapes=list(scratch),
        compiler_params=pltpu.CompilerParams(vmem_limit_bytes=limit),
        cost_estimate=pl.CostEstimate(flops=cost * 10**9, bytes_accessed=MIB, transcendentals=0),
    )(*args)


def split_three(column):
    first = column.astype(jnp.bfloat16)
    left = column - first.astype(jnp.float32)
    second = left.astype(jnp.bfloat16)
    third = (left - second.astype(jnp.float32)).astype(jnp.bfloat16)
    lane = lax.broadcasted_iota(jnp.int32, (column.shape[0], LANES), 1)
    wide = jnp.where(lane == 0, first.astype(jnp.float32), 0.0)
    wide = jnp.where(lane == 1, second.astype(jnp.float32), wide)
    return jnp.where(lane == 2, third.astype(jnp.float32), wide).astype(jnp.bfloat16)


def angle_kernel(lengths_ref, cosine_ref, sine_ref):
    count, width = cosine_ref.shape
    lane = lax.broadcasted_iota(jnp.int32, (1, width), 1)
    step = lax.rem(lane, width // 2).astype(jnp.float32)
    frequency = jnp.exp(step * (-2.0 / width * math.log(rope_base)))
    angles = jnp.concatenate(
        [lengths_ref[i].astype(jnp.float32) * frequency for i in range(count)], axis=0
    )
    cosine_ref[...] = jnp.cos(angles)
    sine = jnp.sin(angles)
    sine_ref[...] = jnp.where(lane < width // 2, -sine, sine)


def project_kernel(_, *refs):
    *block_refs, gain_ref, wq_ref, wk_ref, wv_ref, out_ref, stream_ref = refs[:-3]
    rows_ref, sums_ref, packed_ref = refs[-3:]
    place = lax.axis_index("tp")
    own = block_refs[0].shape[0]
    for k, block_ref in enumerate(block_refs):
        start = pl.multiple_of((place ^ k) * own, own)
        rows_ref[pl.ds(start, own), :] = block_ref[...].astype(jnp.float32)
    rows = rows_ref[...]
    stream_ref[...] = rows.astype(jnp.bfloat16)
    squares = jnp.sum(rows * rows, axis=1, keepdims=True)
    scaled = (rows * gain_ref[...]).astype(jnp.bfloat16)
    count = rows.shape[0]
    groups = 0
    for w_ref in (wq_ref, wk_ref, wv_ref):
        product = jnp.dot(scaled, w_ref[...], preferred_element_type=jnp.float32)
        for at in range(0, w_ref.shape[1], LANES):
            sums_ref[groups * count : (groups + 1) * count, :] = product[:, at : at + LANES]
            groups += 1
    sums_ref[groups * count :, :] = split_three(squares).astype(jnp.float32)
    groups += 1
    devices, depth, _ = out_ref.shape
    each = count // devices
    queries = wq_ref.shape[1] // LANES
    packed_ref[...] = jnp.zeros_like(packed_ref)
    for n in range(each):
        for g in range(groups):
            row = packed_row(n, g, each, queries, groups)
            packed_ref[pl.ds(row, devices, stride=depth), :] = sums_ref[
                pl.ds(g * count + n, devices, stride=each), :
            ]
    out_ref[...] = packed_ref[...].reshape(out_ref.shape).astype(jnp.bfloat16)


def packed_row(n, g, each, queries, groups):
    if g < queries:
        return n * queries + g
    return each * queries + n * (groups - queries) + g - queries


def attend_kernel(
    lengths_ref, got_ref, cosine_ref, sine_ref, keys_ref, values_ref, out_ref
):
    tp_count = KV_HEADS
    devices, depth, width = got_ref.shape
    each, window, _ = keys_ref.shape
    groups = GROUP + 3
    total = jnp.sum(
        got_ref[...].astype(jnp.float32).reshape(devices // tp_count, tp_count, depth, width),
        axis=0,
    )
    factor = HEAD_DIM ** (-0.5)
    scores, own_scores, own_values = [], [], []
    for n in range(each):
        cosine, sine = cosine_ref[n : n + 1, :], sine_ref[n : n + 1, :]
        tail = packed_row(n, GROUP, each, GROUP, groups)
        squares = jnp.sum(total[0, tail + 2 : tail + 3, :], axis=1, keepdims=True)
        inverse = lax.rsqrt(squares / D + epsilon)
        usable = lax.broadcasted_iota(jnp.int32, (GROUP, window), 1) < lengths_ref[n]
        for h in range(tp_count):
            query = total[h, n * GROUP : (n + 1) * GROUP, :]
            key = total[h, tail : tail + 1, :]
            query = query * cosine + pltpu.roll(query, width // 2, 1) * sine
            key = key * cosine + pltpu.roll(key, width // 2, 1) * sine
            query = query.astype(jnp.bfloat16)
            key = key.astype(jnp.bfloat16).astype(jnp.float32)
            score = lax.dot_general(
                query,
                keys_ref[n, :, h * width : (h + 1) * width],
                (((1,), (1,)), ((), ())),
                preferred_element_type=jnp.float32,
            )
            scores.append(jnp.where(usable, score * (inverse * factor), -jnp.inf))
            own_scores.append(
                jnp.sum(query.astype(jnp.float32) * key, axis=1, keepdims=True)
                * (inverse * inverse * factor)
            )
            value = (total[h, tail + 1 : tail + 2, :] * inverse).astype(jnp.bfloat16)
            own_values.append(value.astype(jnp.float32))
    scores, own_scores = jnp.concatenate(scores, axis=0), jnp.concatenate(own_scores, axis=0)
    highest = jnp.maximum(jnp.max(scores, axis=1, keepdims=True), own_scores)
    weights, own_weights = jnp.exp(scores - highest), jnp.exp(own_scores - highest)
    denominator = jnp.sum(weights, axis=1, keepdims=True) + own_weights
    chances = weights.astype(jnp.bfloat16)
    for n in range(each):
        for h in range(tp_count):
            at = (n * tp_count + h) * GROUP
            attended = jnp.dot(
                chances[at : at + GROUP],
                values_ref[n, :, h * width : (h + 1) * width],
                preferred_element_type=jnp.float32,
            )
            attended = attended + own_weights[at : at + GROUP] * own_values[n * tp_count + h]
            attended = attended / denominator[at : at + GROUP]
            for r in range(devices // tp_count):
                out_ref[r * tp_count + h, n * GROUP : (n + 1) * GROUP, :] = attended.astype(
                    jnp.bfloat16
                )


def output_kernel(heads_ref, w_ref, attended_ref, out_ref, heads_wide_ref):
    count = attended_ref.shape[0]
    groups = w_ref.shape[0] // LANES
    heads_wide_ref[...] = heads_ref[...].astype(jnp.float32).reshape(heads_wide_ref.shape)
    for g in range(groups):
        attended_ref[:, g * LANES : (g + 1) * LANES] = heads_wide_ref[
            pl.ds(g, count, stride=groups), :
        ].astype(jnp.bfloat16)
    output_dots(attended_ref, w_ref, out_ref, 0)


def more_output_kernel(begin, attended_ref, w_ref, out_ref):
    output_dots(attended_ref, w_ref, out_ref, begin)


def output_dots(attended_ref, w_ref, out_ref, begin):
    for part in chunks(out_ref.shape[1]):
        out_ref[:, part] = jnp.dot(
            attended_ref[...],
            w_ref[:, begin + part.start : begin + part.stop],
            preferred_element_type=jnp.float32,
        ).astype(jnp.bfloat16)


def live_column(served_ref, count):
    row = lax.broadcasted_iota(jnp.int32, (count, count), 0)
    column = lax.broadcasted_iota(jnp.int32, (count, count), 1)
    return jnp.sum(
        jnp.where(row == column, served_ref[...], 0).astype(jnp.float32), axis=1, keepdims=True
    )


def middle_part(live, stream_ref, term_refs, gain_ref, at, middle_ref, rows_ref):
    width = term_refs[0].shape[1]
    part = slice(at, at + width)
    attn = term_refs[0][...].astype(jnp.float32) + term_refs[1][...].astype(jnp.float32)
    rows = (stream_ref[:, part].astype(jnp.float32) + live * attn).astype(jnp.bfloat16)
    rows = rows.astype(jnp.float32)
    rows_ref[...] = rows
    own = middle_ref.shape[0]
    start = pl.multiple_of(lax.axis_index("tp") * own, own)
    middle_ref[...] = rows_ref[pl.ds(start, own), :].astype(jnp.bfloat16)
    squares = jnp.sum(rows * rows, axis=1, keepdims=True)
    return (rows * gain_ref[:, part]).astype(jnp.bfloat16), squares


def middle_kernel(*refs):
    served_ref, stream_ref, here_ref, far_ref, gain_ref, wg_ref, wu_ref, *refs = refs
    scaled_ref, squares_ref, partial_ref, middle_ref, live_ref, rows_ref, live_rows_ref = refs
    live = live_column(served_ref, stream_ref.shape[0])
    own = middle_ref.shape[0]
    start = pl.multiple_of(lax.axis_index("tp") * own, own)
    live_rows_ref[...] = jnp.broadcast_to(live, live_rows_ref.shape)
    live_ref[...] = live_rows_ref[pl.ds(start, own), :]
    scaled_ref[...], squares = middle_part(
        live, stream_ref, (here_ref, far_ref), gain_ref, 0, middle_ref, rows_ref
    )
    squares_ref[...] = jnp.broadcast_to(squares, squares_ref.shape)
    part_dots(scaled_ref, wg_ref, wu_ref, partial_ref, 0, ())


def more_middle_kernel(*refs):
    served_ref, stream_ref, here_ref, far_ref, gain_ref, wg_ref, wu_ref, *refs = refs
    before_ref, squares_ref, partial_ref, scaled_ref, tail_ref, send_ref, middle_ref, rows_ref = refs
    live = live_column(served_ref, stream_ref.shape[0])
    width = before_ref.shape[1]
    scaled, squares = middle_part(
        live, stream_ref, (here_ref, far_ref), gain_ref, width, middle_ref, rows_ref
    )
    scaled_ref[:, :width] = before_ref[...]
    scaled_ref[:, width:] = scaled
    wide = partial_ref.shape[1]
    part_dots(scaled_ref, wg_ref, wu_ref, send_ref, width, (partial_ref,))
    tail = split_three(squares + squares_ref[:, :1])
    send_ref[:, wide:] = tail
    tail_ref[...] = tail.astype(jnp.float32)


def part_dots(scaled_ref, wg_ref, wu_ref, out_ref, at, before_refs):
    side = 1 - lax.rem(lax.axis_index("role"), 2)
    size = out_ref.shape[1] // (4 * LANES) * 2 * LANES
    depth = scaled_ref.shape[1] - at
    scaled = scaled_ref[:, at:]
    for w_ref, base in ((wg_ref, 0), (wu_ref, size)):
        for step in range(0, size, CHUNK):
            count = min(CHUNK, size - step)
            start = pl.multiple_of(side * (w_ref.shape[1] // 2) + step, LANES)
            part = slice(base + step, base + step + count)
            product = jnp.dot(
                scaled,
                w_ref[at : at + depth, pl.ds(start, count)],
                preferred_element_type=jnp.float32,
            )
            for before_ref in before_refs:
                product = product + before_ref[:, part]
            out_ref[:, part] = product.astype(out_ref.dtype)


def piece_kernel(theirs, begin, size, scaled_ref, wg_ref, wu_ref, *refs):
    half = lax.rem(lax.axis_index("role"), 2)
    side = 1 - half if theirs else half
    piece_dots(scaled_ref, wg_ref, wu_ref, refs[-1], side, begin, size)


def piece_dots(scaled_ref, wg_ref, wu_ref, out_ref, side, begin, size):
    scaled = scaled_ref[...]
    first = side * (wg_ref.shape[1] // 2) + begin
    for w_ref, base in ((wg_ref, 0), (wu_ref, size)):
        for at in range(0, size, CHUNK):
            step = min(CHUNK, size - at)
            start = pl.multiple_of(first + at, LANES)
            out_ref[:, base + at : base + at + step] = jnp.dot(
                scaled, w_ref[:, pl.ds(start, step)], preferred_element_type=jnp.float32
            ).astype(out_ref.dtype)


def pair_tail_kernel(keep_ref, tail_ref, got_ref, out_ref):
    wide = keep_ref.shape[1]
    out_ref[:, :wide] = (keep_ref[...] + got_ref[:, :wide].astype(jnp.float32)).astype(
        jnp.bfloat16
    )
    squares = jnp.sum(
        tail_ref[...] + got_ref[:, wide:].astype(jnp.float32), axis=1, keepdims=True
    )
    out_ref[:, wide:] = split_three(squares)


def pair_kernel(keep_ref, got_ref, out_ref):
    out_ref[...] = (
        keep_ref[...].astype(jnp.float32) + got_ref[...].astype(jnp.float32)
    ).astype(jnp.bfloat16)


def first_hidden_kernel(own_ref, got_ref, hidden_ref, inverse_ref):
    wide = 2 * hidden_ref.shape[1]
    squares = jnp.sum(
        own_ref[:, wide:].astype(jnp.float32) + got_ref[:, wide:].astype(jnp.float32),
        axis=1,
        keepdims=True,
    )
    inverse = lax.rsqrt(squares / D + epsilon)
    inverse_ref[...] = jnp.broadcast_to(inverse, inverse_ref.shape)
    gated(own_ref, got_ref, inverse, hidden_ref)


def hidden_kernel(own_ref, got_ref, inverse_ref, _, hidden_ref):
    gated(own_ref, got_ref, inverse_ref[:, :1], hidden_ref)


def gated(own_ref, got_ref, inverse, hidden_ref):
    size = hidden_ref.shape[1]
    total = own_ref[:, : 2 * size].astype(jnp.float32) + got_ref[:, : 2 * size].astype(jnp.float32)
    total = total * inverse
    gate, up = total[:, :size], total[:, size:]
    hidden_ref[...] = (gate / (1.0 + jnp.exp(-gate)) * up).astype(jnp.bfloat16)


def down_dots(theirs, begin, hidden_ref, w_ref, part):
    half = lax.rem(lax.axis_index("role"), 2)
    side = 1 - half if theirs else half
    start = pl.multiple_of(side * (w_ref.shape[0] // 2) + begin, LANES)
    return jnp.dot(
        hidden_ref[...],
        w_ref[pl.ds(start, hidden_ref.shape[1]), part],
        preferred_element_type=jnp.float32,
    )


def chunks(width):
    return [slice(at, min(at + CHUNK, width)) for at in range(0, width, CHUNK)]


def down_kernel(theirs, begin, hidden_ref, w_ref, *refs):
    *before_refs, rows_ref = refs
    for part in chunks(w_ref.shape[1]):
        rows = down_dots(theirs, begin, hidden_ref, w_ref, part)
        for before_ref in before_refs:
            rows = rows + before_ref[:, part]
        rows_ref[:, part] = rows


def last_down_kernel(theirs, begin, hidden_ref, w_ref, before_ref, *refs):
    *out_refs, rows_ref = refs
    place = lax.axis_index("tp")
    own = out_refs[0].shape[0]
    for part in chunks(w_ref.shape[1]):
        rows_ref[:, part] = before_ref[:, part] + down_dots(
            theirs, begin, hidden_ref, w_ref, part
        )
    for k, out_ref in enumerate(out_refs):
        start = pl.multiple_of((place ^ k) * own, own)
        out_ref[...] = rows_ref[pl.ds(start, own), :].astype(jnp.bfloat16)


def local_exchange(
    residual,
    attn_gain,
    w_query,
    w_key,
    w_value,
    w_output,
    cache_keys,
    cache_values,
    lengths,
    served,
    ffn_gain,
    w_gate,
    w_up,
    w_down,
):
    if not exchange_fits(residual, w_query, w_key, w_gate):
        return local(
            residual,
            attn_gain,
            w_query,
            w_key,
            w_value,
            w_output,
            cache_keys,
            cache_values,
            lengths,
            served,
            ffn_gain,
            w_gate,
            w_up,
            w_down,
        )
    tp_count, role_count = lax.axis_size("tp"), lax.axis_size("role")
    devices = tp_count * role_count
    own, features = residual.shape
    rows = own * tp_count
    each = rows // devices
    block = jax.ShapeDtypeStruct((own, features), jnp.bfloat16)

    table = jax.ShapeDtypeStruct((each, HEAD_DIM), jnp.float32)
    cosine, sine = call(angle_kernel, [table] * 2, [lengths], smem=1, cost=COVER[0])
    others = {k: swap(residual, "tp", k) for k in reversed(range(1, tp_count))}
    blocks = [residual] + [others[k] for k in range(1, tp_count)]
    payload = w_query.shape[1] + 2 * w_key.shape[1] + LANES
    depth = -(-each * payload // (LANES * 8)) * 8
    sums, stream = call(
        project_kernel,
        [
            jax.ShapeDtypeStruct((devices, depth, LANES), jnp.bfloat16),
            jax.ShapeDtypeStruct((rows, features), jnp.bfloat16),
        ],
        [cosine, *blocks, attn_gain[None, :], in_vmem(w_query), in_vmem(w_key), in_vmem(w_value)],
        scratch=[
            pltpu.VMEM((rows, features), jnp.float32),
            pltpu.VMEM((rows * payload // LANES, LANES), jnp.float32),
            pltpu.VMEM((devices * depth, LANES), jnp.float32),
        ],
        cost=COVER[1],
    )
    parts = lax.all_to_all(sums, ("role", "tp"), 0, 0)
    (heads,) = call(
        attend_kernel,
        [jax.ShapeDtypeStruct((devices, each * GROUP, LANES), jnp.bfloat16)],
        [lengths, parts, cosine, sine, in_vmem(cache_keys), in_vmem(cache_values)],
        smem=1,
        cost=COVER[2],
    )
    heads = lax.all_to_all(heads, ("role", "tp"), 0, 0)
    piece = jax.ShapeDtypeStruct((rows, features // 2), jnp.bfloat16)
    w_output = in_vmem(w_output)
    attended, attn_0 = call(
        output_kernel,
        [jax.ShapeDtypeStruct((rows, w_output.shape[0]), jnp.bfloat16), piece],
        [heads, w_output],
        scratch=[pltpu.VMEM((rows * GROUP, LANES), jnp.float32)],
        cost=COVER[3],
    )
    got_0 = swap(attn_0, "tp", 1)
    (attn_1,) = call(
        functools.partial(more_output_kernel, features // 2),
        [piece],
        [attended, w_output],
        cost=COVER[3],
    )
    terms = []
    got_1 = swap(attn_1, "tp", 1)
    for value, got in ((attn_0, got_0), (attn_1, got_1)):
        (paired,) = call(pair_kernel, [piece], [value, got])
        terms += [paired, swap(paired, "tp", 2)]
    width = w_gate.shape[1] // 2
    first = -(-width * FIRST_PART // (100 * 2 * LANES)) * 2 * LANES
    sizes = (first, width - first)
    w_gate, w_up, w_down = in_vmem(w_gate), in_vmem(w_up), in_vmem(w_down)
    rows_f32 = jax.ShapeDtypeStruct((rows, features), jnp.float32)
    row_scratch = pltpu.VMEM((rows, features), jnp.float32)

    def wide(size, dtype, more=0):
        return jax.ShapeDtypeStruct((rows, 2 * size + more), dtype)

    def half_of(piece):
        return jax.ShapeDtypeStruct((rows, sizes[piece]), jnp.bfloat16)

    first_args = [served[None, :], stream]
    weight_args = [ffn_gain[None, :], w_gate, w_up]
    half_block = jax.ShapeDtypeStruct((own, features // 2), jnp.bfloat16)
    lane_rows = jax.ShapeDtypeStruct((rows, LANES), jnp.float32)
    half_scratch = pltpu.VMEM((rows, features // 2), jnp.float32)
    scaled_0, squares, partial, middle_0, live = call(
        middle_kernel,
        [
            piece,
            lane_rows,
            wide(sizes[0], jnp.float32),
            half_block,
            jax.ShapeDtypeStruct((own, LANES), jnp.float32),
        ],
        [*first_args, *terms[:2], *weight_args],
        scratch=[half_scratch, pltpu.VMEM((rows, LANES), jnp.float32)],
        cost=COVER[4],
    )
    scaled, tail, send, middle_1 = call(
        more_middle_kernel,
        [
            jax.ShapeDtypeStruct((rows, features), jnp.bfloat16),
            lane_rows,
            wide(sizes[0], jnp.bfloat16, LANES),
            half_block,
        ],
        [*first_args, *terms[2:], *weight_args, scaled_0, squares, partial],
        scratch=[half_scratch],
        cost=COVER[4],
    )
    middle = jnp.concatenate([middle_0, middle_1], axis=1)
    got = swap(send, "role", 1)
    (keep,) = call(
        functools.partial(piece_kernel, False, 0, sizes[0]),
        [wide(sizes[0], jnp.float32)],
        [scaled, w_gate, w_up],
        cost=COVER[5],
    )
    (chip_0,) = call(
        pair_tail_kernel, [wide(sizes[0], jnp.bfloat16, LANES)], [keep, tail, got]
    )
    far_0 = swap(chip_0, "role", 2)
    (send,) = call(
        functools.partial(piece_kernel, True, sizes[0], sizes[1]),
        [wide(sizes[1], jnp.bfloat16)],
        [scaled, w_gate, w_up, chip_0],
        cost=COVER[6],
    )
    got = swap(send, "role", 1)
    (keep,) = call(
        functools.partial(piece_kernel, False, sizes[0], sizes[1]),
        [wide(sizes[1], jnp.float32)],
        [scaled, w_gate, w_up],
        cost=COVER[7],
    )
    (chip_1,) = call(pair_kernel, [wide(sizes[1], jnp.bfloat16)], [keep, got])
    far_1 = swap(chip_1, "role", 2)
    hidden, inverse = call(
        first_hidden_kernel,
        [half_of(0), jax.ShapeDtypeStruct((rows, LANES), jnp.float32)],
        [chip_0, far_0],
    )
    other = swap(hidden, "role", 1)
    (down,) = call(
        functools.partial(down_kernel, False, 0), [rows_f32], [hidden, w_down], cost=COVER[8]
    )
    (down,) = call(
        functools.partial(down_kernel, True, 0), [rows_f32], [other, w_down, down], cost=COVER[8]
    )
    (hidden,) = call(hidden_kernel, [half_of(1)], [chip_1, far_1, inverse, down])
    other = swap(hidden, "role", 1)
    (down,) = call(
        functools.partial(down_kernel, False, sizes[0]),
        [rows_f32],
        [hidden, w_down, down],
        cost=COVER[9],
    )
    terms = call(
        functools.partial(last_down_kernel, True, sizes[0]),
        [block] * tp_count,
        [other, w_down, down],
        scratch=[row_scratch],
        cost=COVER[9],
    )
    terms = [terms[0]] + [swap(terms[k], "tp", k) for k in range(1, tp_count)]
    ffn = terms[0].astype(jnp.float32)
    for term in terms[1:]:
        ffn = ffn + term.astype(jnp.float32)
    return (middle.astype(jnp.float32) + live[:, :1] * ffn).astype(jnp.bfloat16)


def solution(mesh):
    return jax.shard_map(
        local_exchange,
        mesh=mesh,
        in_specs=(
            P(("groups", "tp"), "role"),
            P("role"),
            P("role", "tp"),
            P("role", "tp"),
            P("role", "tp"),
            P("tp", "role"),
            P(("groups", "role", "tp"), None, None),
            P(("groups", "role", "tp"), None, None),
            P(("groups", "role", "tp")),
            P("groups"),
            P("role"),
            P("role", "tp"),
            P("role", "tp"),
            P("tp", "role"),
        ),
        out_specs=P(("groups", "tp"), "role"),
        check_vma=False,
    )
```

profile of v0, /device:TPU:0, one launch (start us, length us, event | category | flops | bytes accessed | tf_op | source)
XLA Modules:
  0.0 67.1 jit_solution(13980062545817801519)
XLA Ops:
  0.0 4.1 %collective-permute-start.1 = (bf16[8,2048]{1,0:T(8,128)(2,1)}, bf16[8,2048]{1,0:T(8,128)(2,1)S(1)}, u32[]{:S(2)}, u32[]{:S(2)}) collective-permute-start(bf16[8,2048]{1,0:T(8,128)(2,1)} %refs_0_.1), channel_id=1, source_target_pairs={{0,2},{1,3},{2,0},{3,1},{4,6},{5,7},{6,4},{7,5},{8,10},{9,11},{10,... | collective-permute-start | bytes 98312 | tf_op jit(solution)/shard_map/ppermute | solution.py:181
  4.2 1.6 %collective-permute-start = (bf16[8,2048]{1,0:T(8,128)(2,1)}, bf16[8,2048]{1,0:T(8,128)(2,1)S(1)}, u32[]{:S(2)}, u32[]{:S(2)}) collective-permute-start(bf16[8,2048]{1,0:T(8,128)(2,1)} %refs_0_.1), channel_id=1, source_target_pairs={{0,1},{1,0},{2,3},{3,2},{4,5},{5,4},{6,7},{7,6},{8,9},{9,8},{10,11... | collective-permute-start | bytes 98312 | tf_op jit(solution)/shard_map/ppermute | solution.py:181
  5.8 0.7 copy-done.11
  6.4 0.6 shard_map.136
  7.1 1.2 %collective-permute-done.refs_1_ = bf16[8,2048]{1,0:T(8,128)(2,1)S(1)} collective-permute-done((bf16[8,2048]{1,0:T(8,128)(2,1)}, bf16[8,2048]{1,0:T(8,128)(2,1)S(1)}, u32[]{:S(2)}, u32[]{:S(2)}) %collective-permute-start) | collective-permute-done | bytes 32800 | tf_op jit(solution)/shard_map/ppermute | solution.py:181
  8.3 3.4 %collective-permute-done.2.refs_3_ = bf16[8,2048]{1,0:T(8,128)(2,1)S(1)} collective-permute-done((bf16[8,2048]{1,0:T(8,128)(2,1)}, bf16[8,2048]{1,0:T(8,128)(2,1)S(1)}, u32[]{:S(2)}, u32[]{:S(2)}) %collective-permute-start.2) | collective-permute-done | bytes 32800 | tf_op jit(solution)/shard_map/ppermute | solution.py:181
  11.7 1.0 %shard_map.137 = (bf16[16,24,128]{2,1,0:T(8,128)(2,1)S(1)}, bf16[32,2048]{1,0:T(8,128)(2,1)S(1)}) custom-call(f32[2,128]{1,0:T(2,128)S(1)} %get-tuple-element.26._.cosine_ref, bf16[8,2048]{1,0:T(8,128)(2,1)S(1)} %copy-done.6, bf16[8,2048]{1,0:T(8,128)(2,1)S(1)} %collective-permute-done.refs_1_, bf16[8,2048]{1,0:T(8,128)(2,1)S(1)} %collective-permute-done.1.refs_2_, ...), custom_call_target="tpu_custom_call" | custom-call | flops 1000000000 | bytes 1048576 | tf_op jit(solution)/shard_map/pallas_call | solution.py:191
  12.8 10.0 %all_to_all.10.got_ref = bf16[16,24,128]{2,1,0:T(8,128)(2,1)S(1)} all-to-all(bf16[16,24,128]{2,1,0:T(8,128)(2,1)S(1)} %get-tuple-element.28), channel_id=1, replica_groups=mesh['groups'=2,'role'=4,'tp'=4] {'role','tp'}, dimensions={0} | all-to-all | bytes 196608 | tf_op jit(solution)/shard_map/all_to_all | solution.py:580
  22.7 1.1 %shard_map.138 = bf16[16,16,128]{2,1,0:T(8,128)(2,1)S(1)} custom-call(s32[2]{0:T(128)S(1)} %copy-done.11, bf16[16,24,128]{2,1,0:T(8,128)(2,1)S(1)} %all_to_all.10.got_ref, f32[2,128]{1,0:T(2,128)S(1)} %get-tuple-element.26._.cosine_ref, f32[2,128]{1,0:T(2,128)S(1)} %get-tuple-element.29.sine_ref, bf16[2,256,512]{2,1,0:T(8,128)(2,1)S(1)} %copy-done.8, ...), custom_call_target="tpu_custom_call" | custom-call | flops 1000000000 | bytes 1048576 | tf_op jit(solution)/shard_map/pallas_call | solution.py:191
  23.9 9.3 %all_to_all.11.heads_ref = bf16[16,16,128]{2,1,0:T(8,128)(2,1)S(1)} all-to-all(bf16[16,16,128]{2,1,0:T(8,128)(2,1)S(1)} %shard_map.138), channel_id=1, replica_groups=mesh['groups'=2,'role'=4,'tp'=4] {'role','tp'}, dimensions={0} | all-to-all | bytes 131072 | tf_op jit(solution)/shard_map/all_to_all | solution.py:588
  33.1 0.5 shard_map.139
  34.0 0.5 shard_map.142.keep_ref
  34.4 1.7 %collective-permute-start.5 = (bf16[32,1024]{1,0:T(8,128)(2,1)S(1)}, bf16[32,1024]{1,0:T(8,128)(2,1)S(1)}, u32[]{:S(2)}, u32[]{:S(2)}) collective-permute-start(bf16[32,1024]{1,0:T(8,128)(2,1)S(1)} %shard_map.142.keep_ref), channel_id=1, source_target_pairs={{0,1},{1,0},{2,3},{3,2},{4,5},{5,4},{6,7},{7,6},{8,9},{9,8},{10,11... | collective-permute-start | bytes 196616 | tf_op jit(solution)/shard_map/ppermute | solution.py:181
  36.1 2.3 %collective-permute-done.3.got_ref = bf16[32,1024]{1,0:T(8,128)(2,1)S(1)} collective-permute-done((bf16[32,1024]{1,0:T(8,128)(2,1)S(1)}, bf16[32,1024]{1,0:T(8,128)(2,1)S(1)}, u32[]{:S(2)}, u32[]{:S(2)}) %collective-permute-start.3) | collective-permute-done | bytes 65568 | tf_op jit(solution)/shard_map/ppermute | solution.py:181
  38.5 0.8 %collective-permute-start.4 = (bf16[32,1024]{1,0:T(8,128)(2,1)S(1)}, bf16[32,1024]{1,0:T(8,128)(2,1)S(1)}, u32[]{:S(2)}, u32[]{:S(2)}) collective-permute-start(bf16[32,1024]{1,0:T(8,128)(2,1)S(1)} %shard_map.140.refs_2_), channel_id=1, source_target_pairs={{0,2},{1,3},{2,0},{3,1},{4,6},{5,7},{6,4},{7,5},{8,10},{9,11},{10,... | collective-permute-start | bytes 196616 | tf_op jit(solution)/shard_map/ppermute | solution.py:181
  39.3 2.3 %collective-permute-start.6 = (bf16[32,1024]{1,0:T(8,128)(2,1)S(1)}, bf16[32,1024]{1,0:T(8,128)(2,1)S(1)}, u32[]{:S(2)}, u32[]{:S(2)}) collective-permute-start(bf16[32,1024]{1,0:T(8,128)(2,1)S(1)} %shard_map.143.refs_2_), channel_id=1, source_target_pairs={{0,2},{1,3},{2,0},{3,1},{4,6},{5,7},{6,4},{7,5},{8,10},{9,11},{10,... | collective-permute-start | bytes 196616 | tf_op jit(solution)/shard_map/ppermute | solution.py:181
  41.5 3.9 %collective-permute-done.4.refs_3_ = bf16[32,1024]{1,0:T(8,128)(2,1)S(1)} collective-permute-done((bf16[32,1024]{1,0:T(8,128)(2,1)S(1)}, bf16[32,1024]{1,0:T(8,128)(2,1)S(1)}, u32[]{:S(2)}, u32[]{:S(2)}) %collective-permute-start.4) | collective-permute-done | bytes 65568 | tf_op jit(solution)/shard_map/ppermute | solution.py:181
  45.5 0.9 %shard_map.141 = (bf16[32,1024]{1,0:T(8,128)(2,1)S(1)}, f32[32,128]{1,0:T(8,128)S(1)}, f32[32,2048]{1,0:T(8,128)S(1)}, bf16[8,1024]{1,0:T(8,128)(2,1)S(1)}, f32[8,128]{1,0:T(8,128)S(1)}) custom-call(s32[1,32]{1,0:T(1,128)S(1)} %bitcast.8, bf16[32,2048]{1,0:T(8,128)(2,1)S(1)} %get-tuple-element.27.refs_1_, bf16[32,1024]{1,0:T(8,128)(2,1)S(1)} %shard_map.140.refs_2_, ...), custom_call_target="tpu_custom_call" | custom-call | flops 10000000000 | bytes 1048576 | tf_op jit(solution)/shard_map/pallas_call | solution.py:191
  46.4 0.9 %shard_map.144 = (bf16[32,2048]{1,0:T(8,128)(2,1)S(1)}, f32[32,128]{1,0:T(8,128)S(1)}, bf16[32,2176]{1,0:T(8,128)(2,1)S(1)}, bf16[8,1024]{1,0:T(8,128)(2,1)S(1)}) custom-call(s32[1,32]{1,0:T(1,128)S(1)} %bitcast.9, bf16[32,2048]{1,0:T(8,128)(2,1)S(1)} %get-tuple-element.27.refs_1_, bf16[32,1024]{1,0:T(8,128)(2,1)S(1)} %shard_map.143.refs_2_, ...), custom_call_target="tpu_custom_call" | custom-call | flops 10000000000 | bytes 1048576 | tf_op jit(solution)/shard_map/pallas_call | solution.py:191
  47.4 1.5 %shard_map.146.keep_ref = f32[32,2048]{1,0:T(8,128)S(1)} custom-call(bf16[32,2048]{1,0:T(8,128)(2,1)S(1)} %get-tuple-element.38.scaled_ref, bf16[2048,3584]{1,0:T(8,128)(2,1)S(1)} %copy-done.1, bf16[2048,3584]{1,0:T(8,128)(2,1)S(1)} %copy-done.2), custom_call_target="tpu_custom_call" | custom-call | flops 10000000000 | bytes 1048576 | tf_op jit(solution)/shard_map/pallas_call | solution.py:191
  49.4 1.2 %shard_map.148 = bf16[32,1536]{1,0:T(8,128)(2,1)S(1)} custom-call(bf16[32,2048]{1,0:T(8,128)(2,1)S(1)} %get-tuple-element.38.scaled_ref, bf16[2048,3584]{1,0:T(8,128)(2,1)S(1)} %copy-done.1, bf16[2048,3584]{1,0:T(8,128)(2,1)S(1)} %copy-done.2, bf16[32,2176]{1,0:T(8,128)(2,1)S(1)} %shard_map.147.refs_0_.own_ref), custom_call_target="tpu_custom_call" | custom-call | flops 10000000000 | bytes 1048576 | tf_op jit(solution)/shard_map/pallas_call | solution.py:191
  50.9 1.2 %shard_map.145.keep_ref = f32[32,1536]{1,0:T(8,128)S(1)} custom-call(bf16[32,2048]{1,0:T(8,128)(2,1)S(1)} %get-tuple-element.38.scaled_ref, bf16[2048,3584]{1,0:T(8,128)(2,1)S(1)} %copy-done.1, bf16[2048,3584]{1,0:T(8,128)(2,1)S(1)} %copy-done.2), custom_call_target="tpu_custom_call" | custom-call | flops 1000000000 | bytes 1048576 | tf_op jit(solution)/shard_map/pallas_call | solution.py:191
  52.1 1.8 %collective-permute-start.9 = (bf16[32,1536]{1,0:T(8,128)(2,1)S(1)}, bf16[32,1536]{1,0:T(8,128)(2,1)S(1)}, u32[]{:S(2)}, u32[]{:S(2)}) collective-permute-start(bf16[32,1536]{1,0:T(8,128)(2,1)S(1)} %shard_map.149.own_ref), channel_id=1, source_target_pairs={{0,8},{4,12},{8,0},{12,4},{1,9},{5,13},{9,1},{13,5},{2,10},{6,14},... | collective-permute-start | bytes 294920 | tf_op jit(solution)/shard_map/ppermute | solution.py:181
  53.9 1.5 %collective-permute-done.10.got_ref = bf16[32,2176]{1,0:T(8,128)(2,1)S(1)} collective-permute-done((bf16[32,2176]{1,0:T(8,128)(2,1)S(1)}, bf16[32,2176]{1,0:T(8,128)(2,1)S(1)}, u32[]{:S(2)}, u32[]{:S(2)}) %collective-permute-start.10) | collective-permute-done | bytes 139296 | tf_op jit(solution)/shard_map/ppermute | solution.py:181
  55.6 0.8 %shard_map.151.refs_0_ = f32[32,2048]{1,0:T(8,128)S(1)} custom-call(bf16[32,1024]{1,0:T(8,128)(2,1)S(1)} %get-tuple-element.42.hidden_ref, bf16[3584,2048]{1,0:T(8,128)(2,1)S(1)} %bitcast.4), custom_call_target="tpu_custom_call" | custom-call | flops 1000000000 | bytes 1048576 | tf_op jit(solution)/shard_map/pallas_call | solution.py:191
  56.8 0.8 %shard_map.152._.refs_0_ = f32[32,2048]{1,0:T(8,128)S(1)} custom-call(bf16[32,1024]{1,0:T(8,128)(2,1)S(1)} %collective-permute-done.11.hidden_ref, bf16[3584,2048]{1,0:T(8,128)(2,1)S(1)} %bitcast.4, f32[32,2048]{1,0:T(8,128)S(1)} %shard_map.151.refs_0_), custom_call_target="tpu_custom_call" | custom-call | flops 1000000000 | bytes 1048576 | tf_op jit(solution)/shard_map/pallas_call | solution.py:191
  58.0 0.6 shard_map.154.before_ref
  59.1 0.7 shard_map.155
  59.8 0.9 %collective-permute-start.14 = (bf16[8,2048]{1,0:T(8,128)(2,1)S(1)}, bf16[8,2048]{1,0:T(8,128)(2,1)S(1)}, u32[]{:S(2)}, u32[]{:S(2)}) collective-permute-start(bf16[8,2048]{1,0:T(8,128)(2,1)S(1)} %get-tuple-element.45), channel_id=1, source_target_pairs={{0,2},{1,3},{2,0},{3,1},{4,6},{5,7},{6,4},{7,5},{8,10},{9,11},{10,... | collective-permute-start | bytes 98312 | tf_op jit(solution)/shard_map/ppermute | solution.py:181
  60.7 3.5 %collective-permute-start.15 = (bf16[8,2048]{1,0:T(8,128)(2,1)S(1)}, bf16[8,2048]{1,0:T(8,128)(2,1)S(1)}, u32[]{:S(2)}, u32[]{:S(2)}) collective-permute-start(bf16[8,2048]{1,0:T(8,128)(2,1)S(1)} %get-tuple-element.46), channel_id=1, source_target_pairs={{0,3},{1,2},{2,1},{3,0},{4,7},{5,6},{6,5},{7,4},{8,11},{9,10},{10,... | collective-permute-start | bytes 98312 | tf_op jit(solution)/shard_map/ppermute | solution.py:181
  64.7 1.7 %collective-permute-done.15 = bf16[8,2048]{1,0:T(8,128)(2,1)S(1)} collective-permute-done((bf16[8,2048]{1,0:T(8,128)(2,1)S(1)}, bf16[8,2048]{1,0:T(8,128)(2,1)S(1)}, u32[]{:S(2)}, u32[]{:S(2)}) %collective-permute-start.15) | collective-permute-done | bytes 32800 | tf_op jit(solution)/shard_map/ppermute | solution.py:181
  66.4 0.7 %add_convert_fusion = bf16[8,2048]{1,0:T(8,128)(2,1)} fusion(bf16[8,2048]{1,0:T(8,128)(2,1)S(1)} %collective-permute-done.15, bf16[8,2048]{1,0:T(8,128)(2,1)S(1)} %collective-permute-done.14, bf16[8,2048]{1,0:T(8,128)(2,1)S(1)} %collective-permute-done.13, bf16[8,2048]{1,0:T(8,128)(2,1)S(1)} %get-tuple-element.43, bf16[8,1024]{1,0:T(8,128)(2,1)S(1)} %get-tuple-element.36, ...), kind=kLoop, calls=%fused_computation | loop fusion | flops 229376 | bytes 196640 | tf_op jit(solution)/shard_map/convert_element_type | solution.py:711
  (59 shorter events, 3.3 us)
Async XLA Ops:
  0.0 11.7 %copy-start.6 = (bf16[8,2048]{1,0:T(8,128)(2,1)S(1)}, bf16[8,2048]{1,0:T(8,128)(2,1)}, u32[]{:S(2)}) copy-start(bf16[8,2048]{1,0:T(8,128)(2,1)} %refs_0_.1) | copy-start | bytes 98308
  0.0 11.7 %copy-start.5 = (bf16[2048,128]{1,0:T(8,128)(2,1)S(1)}, bf16[2048,128]{1,0:T(8,128)(2,1)}, u32[]{:S(2)}) copy-start(bf16[2048,128]{1,0:T(8,128)(2,1)} %refs_7_.1) | copy-start | bytes 1572868
  0.0 11.7 %copy-start.4 = (bf16[2048,128]{1,0:T(8,128)(2,1)S(1)}, bf16[2048,128]{1,0:T(8,128)(2,1)}, u32[]{:S(2)}) copy-start(bf16[2048,128]{1,0:T(8,128)(2,1)} %refs_6_.3) | copy-start | bytes 1572868
  0.0 11.7 %copy-start.3 = (bf16[2048,1024]{1,0:T(8,128)(2,1)S(1)}, bf16[2048,1024]{1,0:T(8,128)(2,1)}, u32[]{:S(2)}) copy-start(bf16[2048,1024]{1,0:T(8,128)(2,1)} %refs_5_.3) | copy-start | bytes 12582916
  0.0 11.7 %copy-start.7 = (f32[2048]{0:T(1024)S(1)}, f32[2048]{0:T(1024)}, u32[]{:S(2)}) copy-start(f32[2048]{0:T(1024)} %param.15) | copy-start | bytes 24580
  0.0 22.7 %copy-start.9 = (bf16[2,256,512]{2,1,0:T(8,128)(2,1)S(1)}, bf16[2,256,512]{2,1,0:T(8,128)(2,1)}, u32[]{:S(2)}) copy-start(bf16[2,256,512]{2,1,0:T(8,128)(2,1)} %values_ref.1) | copy-start | bytes 1572868
  0.0 22.7 %copy-start.8 = (bf16[2,256,512]{2,1,0:T(8,128)(2,1)S(1)}, bf16[2,256,512]{2,1,0:T(8,128)(2,1)}, u32[]{:S(2)}) copy-start(bf16[2,256,512]{2,1,0:T(8,128)(2,1)} %keys_ref.1) | copy-start | bytes 1572868
  0.0 33.1 %copy-start = (bf16[1024,2048]{1,0:T(8,128)(2,1)S(1)}, bf16[1024,2048]{1,0:T(8,128)(2,1)}, u32[]{:S(2)}) copy-start(bf16[1024,2048]{1,0:T(8,128)(2,1)} %w_ref.7) | copy-start | bytes 12582916
  0.0 7.0 %collective-permute-start.1 = (bf16[8,2048]{1,0:T(8,128)(2,1)}, bf16[8,2048]{1,0:T(8,128)(2,1)S(1)}, u32[]{:S(2)}, u32[]{:S(2)}) collective-permute-start(bf16[8,2048]{1,0:T(8,128)(2,1)} %refs_0_.1), channel_id=1, source_target_pairs={{0,2},{1,3},{2,0},{3,1},{4,6},{5,7},{6,4},{7,5},{8,10},{9,11},{10,... | collective-permute-start | bytes 98312 | tf_op jit(solution)/shard_map/ppermute | solution.py:181
  4.2 4.1 %collective-permute-start = (bf16[8,2048]{1,0:T(8,128)(2,1)}, bf16[8,2048]{1,0:T(8,128)(2,1)S(1)}, u32[]{:S(2)}, u32[]{:S(2)}) collective-permute-start(bf16[8,2048]{1,0:T(8,128)(2,1)} %refs_0_.1), channel_id=1, source_target_pairs={{0,1},{1,0},{2,3},{3,2},{4,5},{5,4},{6,7},{7,6},{8,9},{9,8},{10,11... | collective-permute-start | bytes 98312 | tf_op jit(solution)/shard_map/ppermute | solution.py:181
  5.8 5.9 %collective-permute-start.2 = (bf16[8,2048]{1,0:T(8,128)(2,1)}, bf16[8,2048]{1,0:T(8,128)(2,1)S(1)}, u32[]{:S(2)}, u32[]{:S(2)}) collective-permute-start(bf16[8,2048]{1,0:T(8,128)(2,1)} %refs_0_.1), channel_id=1, source_target_pairs={{0,3},{1,2},{2,1},{3,0},{4,7},{5,6},{6,5},{7,4},{8,11},{9,10},{10,... | collective-permute-start | bytes 98312 | tf_op jit(solution)/shard_map/ppermute | solution.py:181
  6.4 39.1 %copy-start.2 = (bf16[2048,3584]{1,0:T(8,128)(2,1)S(1)}, bf16[2048,3584]{1,0:T(8,128)(2,1)}, u32[]{:S(2)}) copy-start(bf16[2048,3584]{1,0:T(8,128)(2,1)} %wu_ref.5) | copy-start | bytes 44040196
  7.0 38.5 %copy-start.1 = (bf16[2048,3584]{1,0:T(8,128)(2,1)S(1)}, bf16[2048,3584]{1,0:T(8,128)(2,1)}, u32[]{:S(2)}) copy-start(bf16[2048,3584]{1,0:T(8,128)(2,1)} %wg_ref.5) | copy-start | bytes 44040196
  7.0 38.5 %copy-start.10 = (f32[2048]{0:T(1024)S(1)}, f32[2048]{0:T(1024)}, u32[]{:S(2)}) copy-start(f32[2048]{0:T(1024)} %param.24) | copy-start | bytes 24580
  7.0 38.5 %copy-start.12 = (s32[32]{0:T(128)S(1)}, s32[32]{0:T(128)}, u32[]{:S(2)}) copy-start(s32[32]{0:T(128)} %param.23) | copy-start | bytes 388
  33.6 4.8 %collective-permute-start.3 = (bf16[32,1024]{1,0:T(8,128)(2,1)S(1)}, bf16[32,1024]{1,0:T(8,128)(2,1)S(1)}, u32[]{:S(2)}, u32[]{:S(2)}) collective-permute-start(bf16[32,1024]{1,0:T(8,128)(2,1)S(1)} %get-tuple-element.30.keep_ref), channel_id=1, source_target_pairs={{0,1},{1,0},{2,3},{3,2},{4,5},{5,4},{6,7},{7,6},{8,9},{9,8},{10,11... | collective-permute-start | bytes 196616 | tf_op jit(solution)/shard_map/ppermute | solution.py:181
  34.4 4.8 %collective-permute-start.5 = (bf16[32,1024]{1,0:T(8,128)(2,1)S(1)}, bf16[32,1024]{1,0:T(8,128)(2,1)S(1)}, u32[]{:S(2)}, u32[]{:S(2)}) collective-permute-start(bf16[32,1024]{1,0:T(8,128)(2,1)S(1)} %shard_map.142.keep_ref), channel_id=1, source_target_pairs={{0,1},{1,0},{2,3},{3,2},{4,5},{5,4},{6,7},{7,6},{8,9},{9,8},{10,11... | collective-permute-start | bytes 196616 | tf_op jit(solution)/shard_map/ppermute | solution.py:181
  38.5 7.0 %collective-permute-start.4 = (bf16[32,1024]{1,0:T(8,128)(2,1)S(1)}, bf16[32,1024]{1,0:T(8,128)(2,1)S(1)}, u32[]{:S(2)}, u32[]{:S(2)}) collective-permute-start(bf16[32,1024]{1,0:T(8,128)(2,1)S(1)} %shard_map.140.refs_2_), channel_id=1, source_target_pairs={{0,2},{1,3},{2,0},{3,1},{4,6},{5,7},{6,4},{7,5},{8,10},{9,11},{10,... | collective-permute-start | bytes 196616 | tf_op jit(solution)/shard_map/ppermute | solution.py:181
  39.3 7.1 %collective-permute-start.6 = (bf16[32,1024]{1,0:T(8,128)(2,1)S(1)}, bf16[32,1024]{1,0:T(8,128)(2,1)S(1)}, u32[]{:S(2)}, u32[]{:S(2)}) collective-permute-start(bf16[32,1024]{1,0:T(8,128)(2,1)S(1)} %shard_map.143.refs_2_), channel_id=1, source_target_pairs={{0,2},{1,3},{2,0},{3,1},{4,6},{5,7},{6,4},{7,5},{8,10},{9,11},{10,... | collective-permute-start | bytes 196616 | tf_op jit(solution)/shard_map/ppermute | solution.py:181
  47.3 1.6 %collective-permute-start.7 = (bf16[32,2176]{1,0:T(8,128)(2,1)S(1)}, bf16[32,2176]{1,0:T(8,128)(2,1)S(1)}, u32[]{:S(2)}, u32[]{:S(2)}) collective-permute-start(bf16[32,2176]{1,0:T(8,128)(2,1)S(1)} %get-tuple-element.40), channel_id=1, source_target_pairs={{0,4},{4,0},{8,12},{12,8},{1,5},{5,1},{9,13},{13,9},{2,6},{6,2},{1... | collective-permute-start | bytes 417800 | tf_op jit(solution)/shard_map/ppermute | solution.py:181
  49.1 6.3 %collective-permute-start.10 = (bf16[32,2176]{1,0:T(8,128)(2,1)S(1)}, bf16[32,2176]{1,0:T(8,128)(2,1)S(1)}, u32[]{:S(2)}, u32[]{:S(2)}) collective-permute-start(bf16[32,2176]{1,0:T(8,128)(2,1)S(1)} %shard_map.147.refs_0_.own_ref), channel_id=1, source_target_pairs={{0,8},{4,12},{8,0},{12,4},{1,9},{5,13},{9,1},{13,5},{2,10},{6,14},... | collective-permute-start | bytes 417800 | tf_op jit(solution)/shard_map/ppermute | solution.py:181
  49.3 6.2 %slice-start = ((s8[14680064]{0:T(1024)(128)(4,1)}), s8[2097152]{0:T(1024)(128)(4,1)S(1)}, s32[]{:S(2)}) async-start(s8[14680064]{0:T(1024)(128)(4,1)} %bitcast.3), calls=%async_computation.2 | async-start | bytes 4194304
  49.3 6.2 %slice-start.1 = ((s8[14680064]{0:T(1024)(128)(4,1)}), s8[4194304]{0:T(1024)(128)(4,1)S(1)}, s32[]{:S(2)}) async-start(s8[14680064]{0:T(1024)(128)(4,1)} %bitcast.3), calls=%async_computation.3 | async-start | bytes 8388608
  49.4 6.2 %slice-start.2 = ((s8[14680064]{0:T(1024)(128)(4,1)}), s8[4194304]{0:T(1024)(128)(4,1)S(1)}, s32[]{:S(2)}) async-start(s8[14680064]{0:T(1024)(128)(4,1)} %bitcast.3), calls=%async_computation.4 | async-start | bytes 8388608
  50.5 5.1 %slice-start.3 = ((s8[14680064]{0:T(1024)(128)(4,1)}), s8[4194304]{0:T(1024)(128)(4,1)S(1)}, s32[]{:S(2)}) async-start(s8[14680064]{0:T(1024)(128)(4,1)} %bitcast.3), calls=%async_computation.5 | async-start | bytes 8388608
  50.5 1.5 %collective-permute-start.8 = (bf16[32,1536]{1,0:T(8,128)(2,1)S(1)}, bf16[32,1536]{1,0:T(8,128)(2,1)S(1)}, u32[]{:S(2)}, u32[]{:S(2)}) collective-permute-start(bf16[32,1536]{1,0:T(8,128)(2,1)S(1)} %shard_map.148), channel_id=1, source_target_pairs={{0,4},{4,0},{8,12},{12,8},{1,5},{5,1},{9,13},{13,9},{2,6},{6,2},{1... | collective-permute-start | bytes 294920 | tf_op jit(solution)/shard_map/ppermute | solution.py:181
  52.1 5.6 %collective-permute-start.9 = (bf16[32,1536]{1,0:T(8,128)(2,1)S(1)}, bf16[32,1536]{1,0:T(8,128)(2,1)S(1)}, u32[]{:S(2)}, u32[]{:S(2)}) collective-permute-start(bf16[32,1536]{1,0:T(8,128)(2,1)S(1)} %shard_map.149.own_ref), channel_id=1, source_target_pairs={{0,8},{4,12},{8,0},{12,4},{1,9},{5,13},{9,1},{13,5},{2,10},{6,14},... | collective-permute-start | bytes 294920 | tf_op jit(solution)/shard_map/ppermute | solution.py:181
  55.5 1.3 %collective-permute-start.11 = (bf16[32,1024]{1,0:T(8,128)(2,1)S(1)}, bf16[32,1024]{1,0:T(8,128)(2,1)S(1)}, u32[]{:S(2)}, u32[]{:S(2)}) collective-permute-start(bf16[32,1024]{1,0:T(8,128)(2,1)S(1)} %get-tuple-element.42.hidden_ref), channel_id=1, source_target_pairs={{0,4},{4,0},{8,12},{12,8},{1,5},{5,1},{9,13},{13,9},{2,6},{6,2},{1... | collective-permute-start | bytes 196616 | tf_op jit(solution)/shard_map/ppermute | solution.py:181
  57.8 1.3 %collective-permute-start.12 = (bf16[32,768]{1,0:T(8,128)(2,1)S(1)}, bf16[32,768]{1,0:T(8,128)(2,1)S(1)}, u32[]{:S(2)}, u32[]{:S(2)}) collective-permute-start(bf16[32,768]{1,0:T(8,128)(2,1)S(1)} %shard_map.153.hidden_ref), channel_id=1, source_target_pairs={{0,4},{4,0},{8,12},{12,8},{1,5},{5,1},{9,13},{13,9},{2,6},{6,2},{1... | collective-permute-start | bytes 147464 | tf_op jit(solution)/shard_map/ppermute | solution.py:181
  59.7 4.6 %collective-permute-start.13 = (bf16[8,2048]{1,0:T(8,128)(2,1)S(1)}, bf16[8,2048]{1,0:T(8,128)(2,1)S(1)}, u32[]{:S(2)}, u32[]{:S(2)}) collective-permute-start(bf16[8,2048]{1,0:T(8,128)(2,1)S(1)} %get-tuple-element.44), channel_id=1, source_target_pairs={{0,1},{1,0},{2,3},{3,2},{4,5},{5,4},{6,7},{7,6},{8,9},{9,8},{10,11... | collective-permute-start | bytes 98312 | tf_op jit(solution)/shard_map/ppermute | solution.py:181
  59.8 4.9 %collective-permute-start.14 = (bf16[8,2048]{1,0:T(8,128)(2,1)S(1)}, bf16[8,2048]{1,0:T(8,128)(2,1)S(1)}, u32[]{:S(2)}, u32[]{:S(2)}) collective-permute-start(bf16[8,2048]{1,0:T(8,128)(2,1)S(1)} %get-tuple-element.45), channel_id=1, source_target_pairs={{0,2},{1,3},{2,0},{3,1},{4,6},{5,7},{6,4},{7,5},{8,10},{9,11},{10,... | collective-permute-start | bytes 98312 | tf_op jit(solution)/shard_map/ppermute | solution.py:181
  60.7 5.7 %collective-permute-start.15 = (bf16[8,2048]{1,0:T(8,128)(2,1)S(1)}, bf16[8,2048]{1,0:T(8,128)(2,1)S(1)}, u32[]{:S(2)}, u32[]{:S(2)}) collective-permute-start(bf16[8,2048]{1,0:T(8,128)(2,1)S(1)} %get-tuple-element.46), channel_id=1, source_target_pairs={{0,3},{1,2},{2,1},{3,0},{4,7},{5,6},{6,5},{7,4},{8,11},{9,10},{10,... | collective-permute-start | bytes 98312 | tf_op jit(solution)/shard_map/ppermute | solution.py:181
  (1 other events, 0.7 us)
where the time goes:
time: 67.3 us; the launch traced here: 67.1 us
  blocking collectives  19.2 us (29%)
  starting transfers between devices  18 us (27%)
  waiting for transfers between devices  15.3 us (23%)
  Pallas kernels  12.7 us (19%)
  local copies, waits for them, and re-layouts  0.84 us (1%)
  other arithmetic  0.69 us (1%)
    ppermute x16, starting transfers between devices, swap(): return lax.ppermute(value, axis, [(i, i ^ distance) for i in range(count)])  18 us
    ppermute x16, waiting for transfers between devices, swap(): return lax.ppermute(value, axis, [(i, i ^ distance) for i in range(count)])  15.3 us
    pallas_call x20, Pallas kernels, call(): pl.pallas_call(kernel, out_shape=outs, in_specs=specs, out_specs=[pl.Bloc...  12.7 us
    all_to_all x1, blocking collectives, local_exchange(): parts = lax.all_to_all(sums, ('role', 'tp'), 0, 0)  9.97 us
    all_to_all x1, blocking collectives, local_exchange(): heads = lax.all_to_all(heads, ('role', 'tp'), 0, 0)  9.27 us
  transfers between devices with their start and end apart: 16, of which 9 were waited for; matrix products, arithmetic and copies ran while one was open for 0% of the time, Pallas kernels for 12%

commit v1 on v0

--- a/solution.py
+++ b/solution.py
@@ -159,7 +159,7 @@
 MIB = 2**20
 COVER = (100, 1, 1, 1, 10, 10, 10, 1, 1, 1)
 CHUNK = 512
-FIRST_PART = 57
+FIRST_PART = 43
 
 
 def exchange_fits(residual, w_query, w_key, w_gate):
@@ -247,7 +247,8 @@
     devices, depth, _ = out_ref.shape
     each = count // devices
     queries = wq_ref.shape[1] // LANES
-    packed_ref[...] = jnp.zeros_like(packed_ref)
+    for row in range(each * groups, depth):
+        packed_ref[pl.ds(row, devices, stride=depth), :] = jnp.zeros((devices, LANES), jnp.float32)
     for n in range(each):
         for g in range(groups):
             row = packed_row(n, g, each, queries, groups)
@@ -306,6 +307,7 @@
     highest = jnp.maximum(jnp.max(scores, axis=1, keepdims=True), own_scores)
     weights, own_weights = jnp.exp(scores - highest), jnp.exp(own_scores - highest)
     denominator = jnp.sum(weights, axis=1, keepdims=True) + own_weights
+    shrink = 1.0 / denominator
     chances = weights.astype(jnp.bfloat16)
     for n in range(each):
         for h in range(tp_count):
@@ -316,7 +318,7 @@
                 preferred_element_type=jnp.float32,
             )
             attended = attended + own_weights[at : at + GROUP] * own_values[n * tp_count + h]
-            attended = attended / denominator[at : at + GROUP]
+            attended = attended * shrink[at : at + GROUP]
             for r in range(devices // tp_count):
                 out_ref[r * tp_count + h, n * GROUP : (n + 1) * GROUP, :] = attended.astype(
                     jnp.bfloat16
@@ -665,7 +667,7 @@
     (send,) = call(
         functools.partial(piece_kernel, True, sizes[0], sizes[1]),
         [wide(sizes[1], jnp.bfloat16)],
-        [scaled, w_gate, w_up, chip_0],
+        [scaled, w_gate, w_up],
         cost=COVER[6],
     )
     got = swap(send, "role", 1)

time: 67.3 us -> 67.3 us (level)
  no operation moved by 1% of the time
where the time goes in v1:
time: 67.3 us; the launch traced here: 67.1 us
  blocking collectives  19.2 us (29%)
  starting transfers between devices  18 us (27%)
  waiting for transfers between devices  15.3 us (23%)
  Pallas kernels  12.7 us (19%)
  local copies, waits for them, and re-layouts  0.84 us (1%)
  other arithmetic  0.69 us (1%)
    ppermute x16, starting transfers between devices, swap(): return lax.ppermute(value, axis, [(i, i ^ distance) for i in range(count)])  18 us
    ppermute x16, waiting for transfers between devices, swap(): return lax.ppermute(value, axis, [(i, i ^ distance) for i in range(count)])  15.3 us
    pallas_call x20, Pallas kernels, call(): pl.pallas_call(kernel, out_shape=outs, in_specs=specs, out_specs=[pl.Bloc...  12.7 us
    all_to_all x1, blocking collectives, local_exchange(): parts = lax.all_to_all(sums, ('role', 'tp'), 0, 0)  9.97 us
    all_to_all x1, blocking collectives, local_exchange(): heads = lax.all_to_all(heads, ('role', 'tp'), 0, 0)  9.27 us
  transfers between devices with their start and end apart: 16, of which 9 were waited for; matrix products, arithmetic and copies ran while one was open for 0% of the time, Pallas kernels for 12%

profile of v1, /device:TPU:0, one launch (start us, length us, event | category | flops | bytes accessed | tf_op | source)
XLA Modules:
  0.0 67.1 jit_solution(12548358503423099423)
XLA Ops:
  0.0 4.1 %collective-permute-start.1 = (bf16[8,2048]{1,0:T(8,128)(2,1)}, bf16[8,2048]{1,0:T(8,128)(2,1)S(1)}, u32[]{:S(2)}, u32[]{:S(2)}) collective-permute-start(bf16[8,2048]{1,0:T(8,128)(2,1)} %refs_0_.1), channel_id=1, source_target_pairs={{0,2},{1,3},{2,0},{3,1},{4,6},{5,7},{6,4},{7,5},{8,10},{9,11},{10,... | collective-permute-start | bytes 98312 | tf_op jit(solution)/shard_map/ppermute | solution.py:181
  4.2 1.6 %collective-permute-start = (bf16[8,2048]{1,0:T(8,128)(2,1)}, bf16[8,2048]{1,0:T(8,128)(2,1)S(1)}, u32[]{:S(2)}, u32[]{:S(2)}) collective-permute-start(bf16[8,2048]{1,0:T(8,128)(2,1)} %refs_0_.1), channel_id=1, source_target_pairs={{0,1},{1,0},{2,3},{3,2},{4,5},{5,4},{6,7},{7,6},{8,9},{9,8},{10,11... | collective-permute-start | bytes 98312 | tf_op jit(solution)/shard_map/ppermute | solution.py:181
  5.8 0.7 copy-done.11
  6.4 0.6 shard_map.136
  7.1 1.2 %collective-permute-done.refs_1_ = bf16[8,2048]{1,0:T(8,128)(2,1)S(1)} collective-permute-done((bf16[8,2048]{1,0:T(8,128)(2,1)}, bf16[8,2048]{1,0:T(8,128)(2,1)S(1)}, u32[]{:S(2)}, u32[]{:S(2)}) %collective-permute-start) | collective-permute-done | bytes 32800 | tf_op jit(solution)/shard_map/ppermute | solution.py:181
  8.3 3.4 %collective-permute-done.2.refs_3_ = bf16[8,2048]{1,0:T(8,128)(2,1)S(1)} collective-permute-done((bf16[8,2048]{1,0:T(8,128)(2,1)}, bf16[8,2048]{1,0:T(8,128)(2,1)S(1)}, u32[]{:S(2)}, u32[]{:S(2)}) %collective-permute-start.2) | collective-permute-done | bytes 32800 | tf_op jit(solution)/shard_map/ppermute | solution.py:181
  11.7 1.0 %shard_map.137 = (bf16[16,24,128]{2,1,0:T(8,128)(2,1)S(1)}, bf16[32,2048]{1,0:T(8,128)(2,1)S(1)}) custom-call(f32[2,128]{1,0:T(2,128)S(1)} %get-tuple-element.26._.cosine_ref, bf16[8,2048]{1,0:T(8,128)(2,1)S(1)} %copy-done.6, bf16[8,2048]{1,0:T(8,128)(2,1)S(1)} %collective-permute-done.refs_1_, bf16[8,2048]{1,0:T(8,128)(2,1)S(1)} %collective-permute-done.1.refs_2_, ...), custom_call_target="tpu_custom_call" | custom-call | flops 1000000000 | bytes 1048576 | tf_op jit(solution)/shard_map/pallas_call | solution.py:191
  12.8 10.0 %all_to_all.10.got_ref = bf16[16,24,128]{2,1,0:T(8,128)(2,1)S(1)} all-to-all(bf16[16,24,128]{2,1,0:T(8,128)(2,1)S(1)} %get-tuple-element.28), channel_id=1, replica_groups=mesh['groups'=2,'role'=4,'tp'=4] {'role','tp'}, dimensions={0} | all-to-all | bytes 196608 | tf_op jit(solution)/shard_map/all_to_all | solution.py:582
  22.7 1.1 %shard_map.138 = bf16[16,16,128]{2,1,0:T(8,128)(2,1)S(1)} custom-call(s32[2]{0:T(128)S(1)} %copy-done.11, bf16[16,24,128]{2,1,0:T(8,128)(2,1)S(1)} %all_to_all.10.got_ref, f32[2,128]{1,0:T(2,128)S(1)} %get-tuple-element.26._.cosine_ref, f32[2,128]{1,0:T(2,128)S(1)} %get-tuple-element.29.sine_ref, bf16[2,256,512]{2,1,0:T(8,128)(2,1)S(1)} %copy-done.8, ...), custom_call_target="tpu_custom_call" | custom-call | flops 1000000000 | bytes 1048576 | tf_op jit(solution)/shard_map/pallas_call | solution.py:191
  23.9 9.3 %all_to_all.11.heads_ref = bf16[16,16,128]{2,1,0:T(8,128)(2,1)S(1)} all-to-all(bf16[16,16,128]{2,1,0:T(8,128)(2,1)S(1)} %shard_map.138), channel_id=1, replica_groups=mesh['groups'=2,'role'=4,'tp'=4] {'role','tp'}, dimensions={0} | all-to-all | bytes 131072 | tf_op jit(solution)/shard_map/all_to_all | solution.py:590
  33.1 0.5 shard_map.139
  34.0 0.5 shard_map.142.keep_ref
  34.4 1.7 %collective-permute-start.5 = (bf16[32,1024]{1,0:T(8,128)(2,1)S(1)}, bf16[32,1024]{1,0:T(8,128)(2,1)S(1)}, u32[]{:S(2)}, u32[]{:S(2)}) collective-permute-start(bf16[32,1024]{1,0:T(8,128)(2,1)S(1)} %shard_map.142.keep_ref), channel_id=1, source_target_pairs={{0,1},{1,0},{2,3},{3,2},{4,5},{5,4},{6,7},{7,6},{8,9},{9,8},{10,11... | collective-permute-start | bytes 196616 | tf_op jit(solution)/shard_map/ppermute | solution.py:181
  36.1 2.3 %collective-permute-done.3.got_ref = bf16[32,1024]{1,0:T(8,128)(2,1)S(1)} collective-permute-done((bf16[32,1024]{1,0:T(8,128)(2,1)S(1)}, bf16[32,1024]{1,0:T(8,128)(2,1)S(1)}, u32[]{:S(2)}, u32[]{:S(2)}) %collective-permute-start.3) | collective-permute-done | bytes 65568 | tf_op jit(solution)/shard_map/ppermute | solution.py:181
  38.5 0.8 %collective-permute-start.4 = (bf16[32,1024]{1,0:T(8,128)(2,1)S(1)}, bf16[32,1024]{1,0:T(8,128)(2,1)S(1)}, u32[]{:S(2)}, u32[]{:S(2)}) collective-permute-start(bf16[32,1024]{1,0:T(8,128)(2,1)S(1)} %shard_map.140.refs_2_), channel_id=1, source_target_pairs={{0,2},{1,3},{2,0},{3,1},{4,6},{5,7},{6,4},{7,5},{8,10},{9,11},{10,... | collective-permute-start | bytes 196616 | tf_op jit(solution)/shard_map/ppermute | solution.py:181
  39.3 2.3 %collective-permute-start.6 = (bf16[32,1024]{1,0:T(8,128)(2,1)S(1)}, bf16[32,1024]{1,0:T(8,128)(2,1)S(1)}, u32[]{:S(2)}, u32[]{:S(2)}) collective-permute-start(bf16[32,1024]{1,0:T(8,128)(2,1)S(1)} %shard_map.143.refs_2_), channel_id=1, source_target_pairs={{0,2},{1,3},{2,0},{3,1},{4,6},{5,7},{6,4},{7,5},{8,10},{9,11},{10,... | collective-permute-start | bytes 196616 | tf_op jit(solution)/shard_map/ppermute | solution.py:181
  41.5 3.9 %collective-permute-done.4.refs_3_ = bf16[32,1024]{1,0:T(8,128)(2,1)S(1)} collective-permute-done((bf16[32,1024]{1,0:T(8,128)(2,1)S(1)}, bf16[32,1024]{1,0:T(8,128)(2,1)S(1)}, u32[]{:S(2)}, u32[]{:S(2)}) %collective-permute-start.4) | collective-permute-done | bytes 65568 | tf_op jit(solution)/shard_map/ppermute | solution.py:181
  45.5 0.9 %shard_map.141 = (bf16[32,1024]{1,0:T(8,128)(2,1)S(1)}, f32[32,128]{1,0:T(8,128)S(1)}, f32[32,2048]{1,0:T(8,128)S(1)}, bf16[8,1024]{1,0:T(8,128)(2,1)S(1)}, f32[8,128]{1,0:T(8,128)S(1)}) custom-call(s32[1,32]{1,0:T(1,128)S(1)} %bitcast.8, bf16[32,2048]{1,0:T(8,128)(2,1)S(1)} %get-tuple-element.27.refs_1_, bf16[32,1024]{1,0:T(8,128)(2,1)S(1)} %shard_map.140.refs_2_, ...), custom_call_target="tpu_custom_call" | custom-call | flops 10000000000 | bytes 1048576 | tf_op jit(solution)/shard_map/pallas_call | solution.py:191
  46.4 0.9 %shard_map.144 = (bf16[32,2048]{1,0:T(8,128)(2,1)S(1)}, f32[32,128]{1,0:T(8,128)S(1)}, bf16[32,2176]{1,0:T(8,128)(2,1)S(1)}, bf16[8,1024]{1,0:T(8,128)(2,1)S(1)}) custom-call(s32[1,32]{1,0:T(1,128)S(1)} %bitcast.9, bf16[32,2048]{1,0:T(8,128)(2,1)S(1)} %get-tuple-element.27.refs_1_, bf16[32,1024]{1,0:T(8,128)(2,1)S(1)} %shard_map.143.refs_2_, ...), custom_call_target="tpu_custom_call" | custom-call | flops 10000000000 | bytes 1048576 | tf_op jit(solution)/shard_map/pallas_call | solution.py:191
  47.4 1.5 %shard_map.148.keep_ref = f32[32,2048]{1,0:T(8,128)S(1)} custom-call(bf16[32,2048]{1,0:T(8,128)(2,1)S(1)} %get-tuple-element.38.scaled_ref, bf16[2048,3584]{1,0:T(8,128)(2,1)S(1)} %copy-done.1, bf16[2048,3584]{1,0:T(8,128)(2,1)S(1)} %copy-done.2), custom_call_target="tpu_custom_call" | custom-call | flops 10000000000 | bytes 1048576 | tf_op jit(solution)/shard_map/pallas_call | solution.py:191
  49.4 1.2 %shard_map.146 = bf16[32,1536]{1,0:T(8,128)(2,1)S(1)} custom-call(bf16[32,2048]{1,0:T(8,128)(2,1)S(1)} %get-tuple-element.38.scaled_ref, bf16[2048,3584]{1,0:T(8,128)(2,1)S(1)} %copy-done.1, bf16[2048,3584]{1,0:T(8,128)(2,1)S(1)} %copy-done.2), custom_call_target="tpu_custom_call" | custom-call | flops 10000000000 | bytes 1048576 | tf_op jit(solution)/shard_map/pallas_call | solution.py:191
  50.9 1.2 %shard_map.145.keep_ref = f32[32,1536]{1,0:T(8,128)S(1)} custom-call(bf16[32,2048]{1,0:T(8,128)(2,1)S(1)} %get-tuple-element.38.scaled_ref, bf16[2048,3584]{1,0:T(8,128)(2,1)S(1)} %copy-done.1, bf16[2048,3584]{1,0:T(8,128)(2,1)S(1)} %copy-done.2), custom_call_target="tpu_custom_call" | custom-call | flops 1000000000 | bytes 1048576 | tf_op jit(solution)/shard_map/pallas_call | solution.py:191
  52.1 1.8 %collective-permute-start.8 = (bf16[32,1536]{1,0:T(8,128)(2,1)S(1)}, bf16[32,1536]{1,0:T(8,128)(2,1)S(1)}, u32[]{:S(2)}, u32[]{:S(2)}) collective-permute-start(bf16[32,1536]{1,0:T(8,128)(2,1)S(1)} %shard_map.147.own_ref), channel_id=1, source_target_pairs={{0,8},{4,12},{8,0},{12,4},{1,9},{5,13},{9,1},{13,5},{2,10},{6,14},... | collective-permute-start | bytes 294920 | tf_op jit(solution)/shard_map/ppermute | solution.py:181
  53.9 1.5 %collective-permute-done.10.got_ref = bf16[32,2176]{1,0:T(8,128)(2,1)S(1)} collective-permute-done((bf16[32,2176]{1,0:T(8,128)(2,1)S(1)}, bf16[32,2176]{1,0:T(8,128)(2,1)S(1)}, u32[]{:S(2)}, u32[]{:S(2)}) %collective-permute-start.10) | collective-permute-done | bytes 139296 | tf_op jit(solution)/shard_map/ppermute | solution.py:181
  55.6 0.8 %shard_map.151.refs_0_ = f32[32,2048]{1,0:T(8,128)S(1)} custom-call(bf16[32,1024]{1,0:T(8,128)(2,1)S(1)} %get-tuple-element.42.hidden_ref, bf16[3584,2048]{1,0:T(8,128)(2,1)S(1)} %bitcast.4), custom_call_target="tpu_custom_call" | custom-call | flops 1000000000 | bytes 1048576 | tf_op jit(solution)/shard_map/pallas_call | solution.py:191
  56.8 0.8 %shard_map.152._.refs_0_ = f32[32,2048]{1,0:T(8,128)S(1)} custom-call(bf16[32,1024]{1,0:T(8,128)(2,1)S(1)} %collective-permute-done.11.hidden_ref, bf16[3584,2048]{1,0:T(8,128)(2,1)S(1)} %bitcast.4, f32[32,2048]{1,0:T(8,128)S(1)} %shard_map.151.refs_0_), custom_call_target="tpu_custom_call" | custom-call | flops 1000000000 | bytes 1048576 | tf_op jit(solution)/shard_map/pallas_call | solution.py:191
  58.0 0.6 shard_map.154.before_ref
  59.1 0.7 shard_map.155
  59.8 0.9 %collective-permute-start.14 = (bf16[8,2048]{1,0:T(8,128)(2,1)S(1)}, bf16[8,2048]{1,0:T(8,128)(2,1)S(1)}, u32[]{:S(2)}, u32[]{:S(2)}) collective-permute-start(bf16[8,2048]{1,0:T(8,128)(2,1)S(1)} %get-tuple-element.45), channel_id=1, source_target_pairs={{0,2},{1,3},{2,0},{3,1},{4,6},{5,7},{6,4},{7,5},{8,10},{9,11},{10,... | collective-permute-start | bytes 98312 | tf_op jit(solution)/shard_map/ppermute | solution.py:181
  60.7 3.5 %collective-permute-start.15 = (bf16[8,2048]{1,0:T(8,128)(2,1)S(1)}, bf16[8,2048]{1,0:T(8,128)(2,1)S(1)}, u32[]{:S(2)}, u32[]{:S(2)}) collective-permute-start(bf16[8,2048]{1,0:T(8,128)(2,1)S(1)} %get-tuple-element.46), channel_id=1, source_target_pairs={{0,3},{1,2},{2,1},{3,0},{4,7},{5,6},{6,5},{7,4},{8,11},{9,10},{10,... | collective-permute-start | bytes 98312 | tf_op jit(solution)/shard_map/ppermute | solution.py:181
  64.7 1.7 %collective-permute-done.15 = bf16[8,2048]{1,0:T(8,128)(2,1)S(1)} collective-permute-done((bf16[8,2048]{1,0:T(8,128)(2,1)S(1)}, bf16[8,2048]{1,0:T(8,128)(2,1)S(1)}, u32[]{:S(2)}, u32[]{:S(2)}) %collective-permute-start.15) | collective-permute-done | bytes 32800 | tf_op jit(solution)/shard_map/ppermute | solution.py:181
  66.4 0.7 %add_convert_fusion = bf16[8,2048]{1,0:T(8,128)(2,1)} fusion(bf16[8,2048]{1,0:T(8,128)(2,1)S(1)} %collective-permute-done.15, bf16[8,2048]{1,0:T(8,128)(2,1)S(1)} %collective-permute-done.14, bf16[8,2048]{1,0:T(8,128)(2,1)S(1)} %collective-permute-done.13, bf16[8,2048]{1,0:T(8,128)(2,1)S(1)} %get-tuple-element.43, bf16[8,1024]{1,0:T(8,128)(2,1)S(1)} %get-tuple-element.36, ...), kind=kLoop, calls=%fused_computation | loop fusion | flops 229376 | bytes 196640 | tf_op jit(solution)/shard_map/convert_element_type | solution.py:713
  (59 shorter events, 3.3 us)
Async XLA Ops:
  0.0 11.7 %copy-start.6 = (bf16[8,2048]{1,0:T(8,128)(2,1)S(1)}, bf16[8,2048]{1,0:T(8,128)(2,1)}, u32[]{:S(2)}) copy-start(bf16[8,2048]{1,0:T(8,128)(2,1)} %refs_0_.1) | copy-start | bytes 98308
  0.0 11.7 %copy-start.5 = (bf16[2048,128]{1,0:T(8,128)(2,1)S(1)}, bf16[2048,128]{1,0:T(8,128)(2,1)}, u32[]{:S(2)}) copy-start(bf16[2048,128]{1,0:T(8,128)(2,1)} %refs_7_.1) | copy-start | bytes 1572868
  0.0 11.7 %copy-start.4 = (bf16[2048,128]{1,0:T(8,128)(2,1)S(1)}, bf16[2048,128]{1,0:T(8,128)(2,1)}, u32[]{:S(2)}) copy-start(bf16[2048,128]{1,0:T(8,128)(2,1)} %refs_6_.3) | copy-start | bytes 1572868
  0.0 11.7 %copy-start.3 = (bf16[2048,1024]{1,0:T(8,128)(2,1)S(1)}, bf16[2048,1024]{1,0:T(8,128)(2,1)}, u32[]{:S(2)}) copy-start(bf16[2048,1024]{1,0:T(8,128)(2,1)} %refs_5_.3) | copy-start | bytes 12582916
  0.0 11.7 %copy-start.7 = (f32[2048]{0:T(1024)S(1)}, f32[2048]{0:T(1024)}, u32[]{:S(2)}) copy-start(f32[2048]{0:T(1024)} %param.15) | copy-start | bytes 24580
  0.0 22.7 %copy-start.9 = (bf16[2,256,512]{2,1,0:T(8,128)(2,1)S(1)}, bf16[2,256,512]{2,1,0:T(8,128)(2,1)}, u32[]{:S(2)}) copy-start(bf16[2,256,512]{2,1,0:T(8,128)(2,1)} %values_ref.1) | copy-start | bytes 1572868
  0.0 22.7 %copy-start.8 = (bf16[2,256,512]{2,1,0:T(8,128)(2,1)S(1)}, bf16[2,256,512]{2,1,0:T(8,128)(2,1)}, u32[]{:S(2)}) copy-start(bf16[2,256,512]{2,1,0:T(8,128)(2,1)} %keys_ref.1) | copy-start | bytes 1572868
  0.0 33.1 %copy-start = (bf16[1024,2048]{1,0:T(8,128)(2,1)S(1)}, bf16[1024,2048]{1,0:T(8,128)(2,1)}, u32[]{:S(2)}) copy-start(bf16[1024,2048]{1,0:T(8,128)(2,1)} %w_ref.7) | copy-start | bytes 12582916
  0.0 7.0 %collective-permute-start.1 = (bf16[8,2048]{1,0:T(8,128)(2,1)}, bf16[8,2048]{1,0:T(8,128)(2,1)S(1)}, u32[]{:S(2)}, u32[]{:S(2)}) collective-permute-start(bf16[8,2048]{1,0:T(8,128)(2,1)} %refs_0_.1), channel_id=1, source_target_pairs={{0,2},{1,3},{2,0},{3,1},{4,6},{5,7},{6,4},{7,5},{8,10},{9,11},{10,... | collective-permute-start | bytes 98312 | tf_op jit(solution)/shard_map/ppermute | solution.py:181
  4.2 4.1 %collective-permute-start = (bf16[8,2048]{1,0:T(8,128)(2,1)}, bf16[8,2048]{1,0:T(8,128)(2,1)S(1)}, u32[]{:S(2)}, u32[]{:S(2)}) collective-permute-start(bf16[8,2048]{1,0:T(8,128)(2,1)} %refs_0_.1), channel_id=1, source_target_pairs={{0,1},{1,0},{2,3},{3,2},{4,5},{5,4},{6,7},{7,6},{8,9},{9,8},{10,11... | collective-permute-start | bytes 98312 | tf_op jit(solution)/shard_map/ppermute | solution.py:181
  5.8 5.9 %collective-permute-start.2 = (bf16[8,2048]{1,0:T(8,128)(2,1)}, bf16[8,2048]{1,0:T(8,128)(2,1)S(1)}, u32[]{:S(2)}, u32[]{:S(2)}) collective-permute-start(bf16[8,2048]{1,0:T(8,128)(2,1)} %refs_0_.1), channel_id=1, source_target_pairs={{0,3},{1,2},{2,1},{3,0},{4,7},{5,6},{6,5},{7,4},{8,11},{9,10},{10,... | collective-permute-start | bytes 98312 | tf_op jit(solution)/shard_map/ppermute | solution.py:181
  6.4 39.1 %copy-start.2 = (bf16[2048,3584]{1,0:T(8,128)(2,1)S(1)}, bf16[2048,3584]{1,0:T(8,128)(2,1)}, u32[]{:S(2)}) copy-start(bf16[2048,3584]{1,0:T(8,128)(2,1)} %wu_ref.5) | copy-start | bytes 44040196
  7.0 38.5 %copy-start.1 = (bf16[2048,3584]{1,0:T(8,128)(2,1)S(1)}, bf16[2048,3584]{1,0:T(8,128)(2,1)}, u32[]{:S(2)}) copy-start(bf16[2048,3584]{1,0:T(8,128)(2,1)} %wg_ref.5) | copy-start | bytes 44040196
  7.0 38.5 %copy-start.10 = (f32[2048]{0:T(1024)S(1)}, f32[2048]{0:T(1024)}, u32[]{:S(2)}) copy-start(f32[2048]{0:T(1024)} %param.24) | copy-start | bytes 24580
  7.0 38.5 %copy-start.12 = (s32[32]{0:T(128)S(1)}, s32[32]{0:T(128)}, u32[]{:S(2)}) copy-start(s32[32]{0:T(128)} %param.23) | copy-start | bytes 388
  33.6 4.8 %collective-permute-start.3 = (bf16[32,1024]{1,0:T(8,128)(2,1)S(1)}, bf16[32,1024]{1,0:T(8,128)(2,1)S(1)}, u32[]{:S(2)}, u32[]{:S(2)}) collective-permute-start(bf16[32,1024]{1,0:T(8,128)(2,1)S(1)} %get-tuple-element.30.keep_ref), channel_id=1, source_target_pairs={{0,1},{1,0},{2,3},{3,2},{4,5},{5,4},{6,7},{7,6},{8,9},{9,8},{10,11... | collective-permute-start | bytes 196616 | tf_op jit(solution)/shard_map/ppermute | solution.py:181
  34.4 4.8 %collective-permute-start.5 = (bf16[32,1024]{1,0:T(8,128)(2,1)S(1)}, bf16[32,1024]{1,0:T(8,128)(2,1)S(1)}, u32[]{:S(2)}, u32[]{:S(2)}) collective-permute-start(bf16[32,1024]{1,0:T(8,128)(2,1)S(1)} %shard_map.142.keep_ref), channel_id=1, source_target_pairs={{0,1},{1,0},{2,3},{3,2},{4,5},{5,4},{6,7},{7,6},{8,9},{9,8},{10,11... | collective-permute-start | bytes 196616 | tf_op jit(solution)/shard_map/ppermute | solution.py:181
  38.5 7.0 %collective-permute-start.4 = (bf16[32,1024]{1,0:T(8,128)(2,1)S(1)}, bf16[32,1024]{1,0:T(8,128)(2,1)S(1)}, u32[]{:S(2)}, u32[]{:S(2)}) collective-permute-start(bf16[32,1024]{1,0:T(8,128)(2,1)S(1)} %shard_map.140.refs_2_), channel_id=1, source_target_pairs={{0,2},{1,3},{2,0},{3,1},{4,6},{5,7},{6,4},{7,5},{8,10},{9,11},{10,... | collective-permute-start | bytes 196616 | tf_op jit(solution)/shard_map/ppermute | solution.py:181
  39.3 7.1 %collective-permute-start.6 = (bf16[32,1024]{1,0:T(8,128)(2,1)S(1)}, bf16[32,1024]{1,0:T(8,128)(2,1)S(1)}, u32[]{:S(2)}, u32[]{:S(2)}) collective-permute-start(bf16[32,1024]{1,0:T(8,128)(2,1)S(1)} %shard_map.143.refs_2_), channel_id=1, source_target_pairs={{0,2},{1,3},{2,0},{3,1},{4,6},{5,7},{6,4},{7,5},{8,10},{9,11},{10,... | collective-permute-start | bytes 196616 | tf_op jit(solution)/shard_map/ppermute | solution.py:181
  47.3 1.6 %collective-permute-start.9 = (bf16[32,2176]{1,0:T(8,128)(2,1)S(1)}, bf16[32,2176]{1,0:T(8,128)(2,1)S(1)}, u32[]{:S(2)}, u32[]{:S(2)}) collective-permute-start(bf16[32,2176]{1,0:T(8,128)(2,1)S(1)} %get-tuple-element.40), channel_id=1, source_target_pairs={{0,4},{4,0},{8,12},{12,8},{1,5},{5,1},{9,13},{13,9},{2,6},{6,2},{1... | collective-permute-start | bytes 417800 | tf_op jit(solution)/shard_map/ppermute | solution.py:181
  49.1 6.3 %collective-permute-start.10 = (bf16[32,2176]{1,0:T(8,128)(2,1)S(1)}, bf16[32,2176]{1,0:T(8,128)(2,1)S(1)}, u32[]{:S(2)}, u32[]{:S(2)}) collective-permute-start(bf16[32,2176]{1,0:T(8,128)(2,1)S(1)} %shard_map.149.own_ref), channel_id=1, source_target_pairs={{0,8},{4,12},{8,0},{12,4},{1,9},{5,13},{9,1},{13,5},{2,10},{6,14},... | collective-permute-start | bytes 417800 | tf_op jit(solution)/shard_map/ppermute | solution.py:181
  49.3 6.2 %slice-start = ((s8[14680064]{0:T(1024)(128)(4,1)}), s8[4194304]{0:T(1024)(128)(4,1)S(1)}, s32[]{:S(2)}) async-start(s8[14680064]{0:T(1024)(128)(4,1)} %bitcast.3), calls=%async_computation.2 | async-start | bytes 8388608
  49.3 6.2 %slice-start.1 = ((s8[14680064]{0:T(1024)(128)(4,1)}), s8[4194304]{0:T(1024)(128)(4,1)S(1)}, s32[]{:S(2)}) async-start(s8[14680064]{0:T(1024)(128)(4,1)} %bitcast.3), calls=%async_computation.3 | async-start | bytes 8388608
  49.4 6.2 %slice-start.2 = ((s8[14680064]{0:T(1024)(128)(4,1)}), s8[4194304]{0:T(1024)(128)(4,1)S(1)}, s32[]{:S(2)}) async-start(s8[14680064]{0:T(1024)(128)(4,1)} %bitcast.3), calls=%async_computation.4 | async-start | bytes 8388608
  50.5 5.1 %slice-start.3 = ((s8[14680064]{0:T(1024)(128)(4,1)}), s8[2097152]{0:T(1024)(128)(4,1)S(1)}, s32[]{:S(2)}) async-start(s8[14680064]{0:T(1024)(128)(4,1)} %bitcast.3), calls=%async_computation.5 | async-start | bytes 4194304
  50.5 1.5 %collective-permute-start.7 = (bf16[32,1536]{1,0:T(8,128)(2,1)S(1)}, bf16[32,1536]{1,0:T(8,128)(2,1)S(1)}, u32[]{:S(2)}, u32[]{:S(2)}) collective-permute-start(bf16[32,1536]{1,0:T(8,128)(2,1)S(1)} %shard_map.146), channel_id=1, source_target_pairs={{0,4},{4,0},{8,12},{12,8},{1,5},{5,1},{9,13},{13,9},{2,6},{6,2},{1... | collective-permute-start | bytes 294920 | tf_op jit(solution)/shard_map/ppermute | solution.py:181
  52.1 5.6 %collective-permute-start.8 = (bf16[32,1536]{1,0:T(8,128)(2,1)S(1)}, bf16[32,1536]{1,0:T(8,128)(2,1)S(1)}, u32[]{:S(2)}, u32[]{:S(2)}) collective-permute-start(bf16[32,1536]{1,0:T(8,128)(2,1)S(1)} %shard_map.147.own_ref), channel_id=1, source_target_pairs={{0,8},{4,12},{8,0},{12,4},{1,9},{5,13},{9,1},{13,5},{2,10},{6,14},... | collective-permute-start | bytes 294920 | tf_op jit(solution)/shard_map/ppermute | solution.py:181
  55.5 1.3 %collective-permute-start.11 = (bf16[32,1024]{1,0:T(8,128)(2,1)S(1)}, bf16[32,1024]{1,0:T(8,128)(2,1)S(1)}, u32[]{:S(2)}, u32[]{:S(2)}) collective-permute-start(bf16[32,1024]{1,0:T(8,128)(2,1)S(1)} %get-tuple-element.42.hidden_ref), channel_id=1, source_target_pairs={{0,4},{4,0},{8,12},{12,8},{1,5},{5,1},{9,13},{13,9},{2,6},{6,2},{1... | collective-permute-start | bytes 196616 | tf_op jit(solution)/shard_map/ppermute | solution.py:181
  57.8 1.3 %collective-permute-start.12 = (bf16[32,768]{1,0:T(8,128)(2,1)S(1)}, bf16[32,768]{1,0:T(8,128)(2,1)S(1)}, u32[]{:S(2)}, u32[]{:S(2)}) collective-permute-start(bf16[32,768]{1,0:T(8,128)(2,1)S(1)} %shard_map.153.hidden_ref), channel_id=1, source_target_pairs={{0,4},{4,0},{8,12},{12,8},{1,5},{5,1},{9,13},{13,9},{2,6},{6,2},{1... | collective-permute-start | bytes 147464 | tf_op jit(solution)/shard_map/ppermute | solution.py:181
  59.7 4.6 %collective-permute-start.13 = (bf16[8,2048]{1,0:T(8,128)(2,1)S(1)}, bf16[8,2048]{1,0:T(8,128)(2,1)S(1)}, u32[]{:S(2)}, u32[]{:S(2)}) collective-permute-start(bf16[8,2048]{1,0:T(8,128)(2,1)S(1)} %get-tuple-element.44), channel_id=1, source_target_pairs={{0,1},{1,0},{2,3},{3,2},{4,5},{5,4},{6,7},{7,6},{8,9},{9,8},{10,11... | collective-permute-start | bytes 98312 | tf_op jit(solution)/shard_map/ppermute | solution.py:181
  59.8 4.9 %collective-permute-start.14 = (bf16[8,2048]{1,0:T(8,128)(2,1)S(1)}, bf16[8,2048]{1,0:T(8,128)(2,1)S(1)}, u32[]{:S(2)}, u32[]{:S(2)}) collective-permute-start(bf16[8,2048]{1,0:T(8,128)(2,1)S(1)} %get-tuple-element.45), channel_id=1, source_target_pairs={{0,2},{1,3},{2,0},{3,1},{4,6},{5,7},{6,4},{7,5},{8,10},{9,11},{10,... | collective-permute-start | bytes 98312 | tf_op jit(solution)/shard_map/ppermute | solution.py:181
  60.7 5.7 %collective-permute-start.15 = (bf16[8,2048]{1,0:T(8,128)(2,1)S(1)}, bf16[8,2048]{1,0:T(8,128)(2,1)S(1)}, u32[]{:S(2)}, u32[]{:S(2)}) collective-permute-start(bf16[8,2048]{1,0:T(8,128)(2,1)S(1)} %get-tuple-element.46), channel_id=1, source_target_pairs={{0,3},{1,2},{2,1},{3,0},{4,7},{5,6},{6,5},{7,4},{8,11},{9,10},{10,... | collective-permute-start | bytes 98312 | tf_op jit(solution)/shard_map/ppermute | solution.py:181
  (1 other events, 0.7 us)

commit v2 on v1

--- a/solution.py
+++ b/solution.py
@@ -158,7 +158,7 @@
 LANES = 128
 MIB = 2**20
 COVER = (100, 1, 1, 1, 10, 10, 10, 1, 1, 1)
-CHUNK = 512
+CHUNK = 1024
 FIRST_PART = 43
 
 
@@ -247,8 +247,7 @@
     devices, depth, _ = out_ref.shape
     each = count // devices
     queries = wq_ref.shape[1] // LANES
-    for row in range(each * groups, depth):
-        packed_ref[pl.ds(row, devices, stride=depth), :] = jnp.zeros((devices, LANES), jnp.float32)
+    packed_ref[...] = jnp.zeros_like(packed_ref)
     for n in range(each):
         for g in range(groups):
             row = packed_row(n, g, each, queries, groups)
@@ -667,7 +666,7 @@
     (send,) = call(
         functools.partial(piece_kernel, True, sizes[0], sizes[1]),
         [wide(sizes[1], jnp.bfloat16)],
-        [scaled, w_gate, w_up],
+        [scaled, w_gate, w_up, chip_0],
         cost=COVER[6],
     )
     got = swap(send, "role", 1)

time: 67.3 us -> 67.3 us (level)
  no operation moved by 1% of the time
where the time goes in v2:
time: 67.3 us; the launch traced here: 67.1 us
  blocking collectives  19.2 us (29%)
  starting transfers between devices  18 us (27%)
  waiting for transfers between devices  15.3 us (23%)
  Pallas kernels  12.7 us (19%)
  local copies, waits for them, and re-layouts  0.84 us (1%)
  other arithmetic  0.69 us (1%)
    ppermute x16, starting transfers between devices, swap(): return lax.ppermute(value, axis, [(i, i ^ distance) for i in range(count)])  18 us
    ppermute x16, waiting for transfers between devices, swap(): return lax.ppermute(value, axis, [(i, i ^ distance) for i in range(count)])  15.3 us
    pallas_call x20, Pallas kernels, call(): pl.pallas_call(kernel, out_shape=outs, in_specs=specs, out_specs=[pl.Bloc...  12.7 us
    all_to_all x1, blocking collectives, local_exchange(): parts = lax.all_to_all(sums, ('role', 'tp'), 0, 0)  9.97 us
    all_to_all x1, blocking collectives, local_exchange(): heads = lax.all_to_all(heads, ('role', 'tp'), 0, 0)  9.27 us
  transfers between devices with their start and end apart: 16, of which 9 were waited for; matrix products, arithmetic and copies ran while one was open for 0% of the time, Pallas kernels for 12%

profile of v2, /device:TPU:0, one launch (start us, length us, event | category | flops | bytes accessed | tf_op | source)
XLA Modules:
  0.0 67.1 jit_solution(1848685304174628895)
XLA Ops:
  0.0 4.1 %collective-permute-start.1 = (bf16[8,2048]{1,0:T(8,128)(2,1)}, bf16[8,2048]{1,0:T(8,128)(2,1)S(1)}, u32[]{:S(2)}, u32[]{:S(2)}) collective-permute-start(bf16[8,2048]{1,0:T(8,128)(2,1)} %refs_0_.1), channel_id=1, source_target_pairs={{0,2},{1,3},{2,0},{3,1},{4,6},{5,7},{6,4},{7,5},{8,10},{9,11},{10,... | collective-permute-start | bytes 98312 | tf_op jit(solution)/shard_map/ppermute | solution.py:181
  4.2 1.6 %collective-permute-start = (bf16[8,2048]{1,0:T(8,128)(2,1)}, bf16[8,2048]{1,0:T(8,128)(2,1)S(1)}, u32[]{:S(2)}, u32[]{:S(2)}) collective-permute-start(bf16[8,2048]{1,0:T(8,128)(2,1)} %refs_0_.1), channel_id=1, source_target_pairs={{0,1},{1,0},{2,3},{3,2},{4,5},{5,4},{6,7},{7,6},{8,9},{9,8},{10,11... | collective-permute-start | bytes 98312 | tf_op jit(solution)/shard_map/ppermute | solution.py:181
  5.8 0.7 copy-done.11
  6.4 0.6 shard_map.136
  7.1 1.2 %collective-permute-done.refs_1_ = bf16[8,2048]{1,0:T(8,128)(2,1)S(1)} collective-permute-done((bf16[8,2048]{1,0:T(8,128)(2,1)}, bf16[8,2048]{1,0:T(8,128)(2,1)S(1)}, u32[]{:S(2)}, u32[]{:S(2)}) %collective-permute-start) | collective-permute-done | bytes 32800 | tf_op jit(solution)/shard_map/ppermute | solution.py:181
  8.3 3.4 %collective-permute-done.2.refs_3_ = bf16[8,2048]{1,0:T(8,128)(2,1)S(1)} collective-permute-done((bf16[8,2048]{1,0:T(8,128)(2,1)}, bf16[8,2048]{1,0:T(8,128)(2,1)S(1)}, u32[]{:S(2)}, u32[]{:S(2)}) %collective-permute-start.2) | collective-permute-done | bytes 32800 | tf_op jit(solution)/shard_map/ppermute | solution.py:181
  11.7 1.0 %shard_map.137 = (bf16[16,24,128]{2,1,0:T(8,128)(2,1)S(1)}, bf16[32,2048]{1,0:T(8,128)(2,1)S(1)}) custom-call(f32[2,128]{1,0:T(2,128)S(1)} %get-tuple-element.26._.cosine_ref, bf16[8,2048]{1,0:T(8,128)(2,1)S(1)} %copy-done.6, bf16[8,2048]{1,0:T(8,128)(2,1)S(1)} %collective-permute-done.refs_1_, bf16[8,2048]{1,0:T(8,128)(2,1)S(1)} %collective-permute-done.1.refs_2_, ...), custom_call_target="tpu_custom_call" | custom-call | flops 1000000000 | bytes 1048576 | tf_op jit(solution)/shard_map/pallas_call | solution.py:191
  12.8 10.0 %all_to_all.10.got_ref = bf16[16,24,128]{2,1,0:T(8,128)(2,1)S(1)} all-to-all(bf16[16,24,128]{2,1,0:T(8,128)(2,1)S(1)} %get-tuple-element.28), channel_id=1, replica_groups=mesh['groups'=2,'role'=4,'tp'=4] {'role','tp'}, dimensions={0} | all-to-all | bytes 196608 | tf_op jit(solution)/shard_map/all_to_all | solution.py:581
  22.7 1.1 %shard_map.138 = bf16[16,16,128]{2,1,0:T(8,128)(2,1)S(1)} custom-call(s32[2]{0:T(128)S(1)} %copy-done.11, bf16[16,24,128]{2,1,0:T(8,128)(2,1)S(1)} %all_to_all.10.got_ref, f32[2,128]{1,0:T(2,128)S(1)} %get-tuple-element.26._.cosine_ref, f32[2,128]{1,0:T(2,128)S(1)} %get-tuple-element.29.sine_ref, bf16[2,256,512]{2,1,0:T(8,128)(2,1)S(1)} %copy-done.8, ...), custom_call_target="tpu_custom_call" | custom-call | flops 1000000000 | bytes 1048576 | tf_op jit(solution)/shard_map/pallas_call | solution.py:191
  23.9 9.3 %all_to_all.11.heads_ref = bf16[16,16,128]{2,1,0:T(8,128)(2,1)S(1)} all-to-all(bf16[16,16,128]{2,1,0:T(8,128)(2,1)S(1)} %shard_map.138), channel_id=1, replica_groups=mesh['groups'=2,'role'=4,'tp'=4] {'role','tp'}, dimensions={0} | all-to-all | bytes 131072 | tf_op jit(solution)/shard_map/all_to_all | solution.py:589
  33.1 0.5 shard_map.139
  34.0 0.5 shard_map.142.keep_ref
  34.4 1.7 %collective-permute-start.5 = (bf16[32,1024]{1,0:T(8,128)(2,1)S(1)}, bf16[32,1024]{1,0:T(8,128)(2,1)S(1)}, u32[]{:S(2)}, u32[]{:S(2)}) collective-permute-start(bf16[32,1024]{1,0:T(8,128)(2,1)S(1)} %shard_map.142.keep_ref), channel_id=1, source_target_pairs={{0,1},{1,0},{2,3},{3,2},{4,5},{5,4},{6,7},{7,6},{8,9},{9,8},{10,11... | collective-permute-start | bytes 196616 | tf_op jit(solution)/shard_map/ppermute | solution.py:181
  36.1 2.3 %collective-permute-done.3.got_ref = bf16[32,1024]{1,0:T(8,128)(2,1)S(1)} collective-permute-done((bf16[32,1024]{1,0:T(8,128)(2,1)S(1)}, bf16[32,1024]{1,0:T(8,128)(2,1)S(1)}, u32[]{:S(2)}, u32[]{:S(2)}) %collective-permute-start.3) | collective-permute-done | bytes 65568 | tf_op jit(solution)/shard_map/ppermute | solution.py:181
  38.5 0.8 %collective-permute-start.4 = (bf16[32,1024]{1,0:T(8,128)(2,1)S(1)}, bf16[32,1024]{1,0:T(8,128)(2,1)S(1)}, u32[]{:S(2)}, u32[]{:S(2)}) collective-permute-start(bf16[32,1024]{1,0:T(8,128)(2,1)S(1)} %shard_map.140.refs_2_), channel_id=1, source_target_pairs={{0,2},{1,3},{2,0},{3,1},{4,6},{5,7},{6,4},{7,5},{8,10},{9,11},{10,... | collective-permute-start | bytes 196616 | tf_op jit(solution)/shard_map/ppermute | solution.py:181
  39.3 2.3 %collective-permute-start.6 = (bf16[32,1024]{1,0:T(8,128)(2,1)S(1)}, bf16[32,1024]{1,0:T(8,128)(2,1)S(1)}, u32[]{:S(2)}, u32[]{:S(2)}) collective-permute-start(bf16[32,1024]{1,0:T(8,128)(2,1)S(1)} %shard_map.143.refs_2_), channel_id=1, source_target_pairs={{0,2},{1,3},{2,0},{3,1},{4,6},{5,7},{6,4},{7,5},{8,10},{9,11},{10,... | collective-permute-start | bytes 196616 | tf_op jit(solution)/shard_map/ppermute | solution.py:181
  41.5 3.9 %collective-permute-done.4.refs_3_ = bf16[32,1024]{1,0:T(8,128)(2,1)S(1)} collective-permute-done((bf16[32,1024]{1,0:T(8,128)(2,1)S(1)}, bf16[32,1024]{1,0:T(8,128)(2,1)S(1)}, u32[]{:S(2)}, u32[]{:S(2)}) %collective-permute-start.4) | collective-permute-done | bytes 65568 | tf_op jit(solution)/shard_map/ppermute | solution.py:181
  45.5 0.9 %shard_map.141 = (bf16[32,1024]{1,0:T(8,128)(2,1)S(1)}, f32[32,128]{1,0:T(8,128)S(1)}, f32[32,2048]{1,0:T(8,128)S(1)}, bf16[8,1024]{1,0:T(8,128)(2,1)S(1)}, f32[8,128]{1,0:T(8,128)S(1)}) custom-call(s32[1,32]{1,0:T(1,128)S(1)} %bitcast.8, bf16[32,2048]{1,0:T(8,128)(2,1)S(1)} %get-tuple-element.27.refs_1_, bf16[32,1024]{1,0:T(8,128)(2,1)S(1)} %shard_map.140.refs_2_, ...), custom_call_target="tpu_custom_call" | custom-call | flops 10000000000 | bytes 1048576 | tf_op jit(solution)/shard_map/pallas_call | solution.py:191
  46.4 0.9 %shard_map.144 = (bf16[32,2048]{1,0:T(8,128)(2,1)S(1)}, f32[32,128]{1,0:T(8,128)S(1)}, bf16[32,2176]{1,0:T(8,128)(2,1)S(1)}, bf16[8,1024]{1,0:T(8,128)(2,1)S(1)}) custom-call(s32[1,32]{1,0:T(1,128)S(1)} %bitcast.9, bf16[32,2048]{1,0:T(8,128)(2,1)S(1)} %get-tuple-element.27.refs_1_, bf16[32,1024]{1,0:T(8,128)(2,1)S(1)} %shard_map.143.refs_2_, ...), custom_call_target="tpu_custom_call" | custom-call | flops 10000000000 | bytes 1048576 | tf_op jit(solution)/shard_map/pallas_call | solution.py:191
  47.4 1.5 %shard_map.146.keep_ref = f32[32,2048]{1,0:T(8,128)S(1)} custom-call(bf16[32,2048]{1,0:T(8,128)(2,1)S(1)} %get-tuple-element.38.scaled_ref, bf16[2048,3584]{1,0:T(8,128)(2,1)S(1)} %copy-done.1, bf16[2048,3584]{1,0:T(8,128)(2,1)S(1)} %copy-done.2), custom_call_target="tpu_custom_call" | custom-call | flops 10000000000 | bytes 1048576 | tf_op jit(solution)/shard_map/pallas_call | solution.py:191
  49.3 1.2 %shard_map.148 = bf16[32,1536]{1,0:T(8,128)(2,1)S(1)} custom-call(bf16[32,2048]{1,0:T(8,128)(2,1)S(1)} %get-tuple-element.38.scaled_ref, bf16[2048,3584]{1,0:T(8,128)(2,1)S(1)} %copy-done.1, bf16[2048,3584]{1,0:T(8,128)(2,1)S(1)} %copy-done.2, bf16[32,2176]{1,0:T(8,128)(2,1)S(1)} %shard_map.147.refs_0_.own_ref), custom_call_target="tpu_custom_call" | custom-call | flops 10000000000 | bytes 1048576 | tf_op jit(solution)/shard_map/pallas_call | solution.py:191
  50.9 1.2 %shard_map.145.keep_ref = f32[32,1536]{1,0:T(8,128)S(1)} custom-call(bf16[32,2048]{1,0:T(8,128)(2,1)S(1)} %get-tuple-element.38.scaled_ref, bf16[2048,3584]{1,0:T(8,128)(2,1)S(1)} %copy-done.1, bf16[2048,3584]{1,0:T(8,128)(2,1)S(1)} %copy-done.2), custom_call_target="tpu_custom_call" | custom-call | flops 1000000000 | bytes 1048576 | tf_op jit(solution)/shard_map/pallas_call | solution.py:191
  52.1 1.8 %collective-permute-start.9 = (bf16[32,1536]{1,0:T(8,128)(2,1)S(1)}, bf16[32,1536]{1,0:T(8,128)(2,1)S(1)}, u32[]{:S(2)}, u32[]{:S(2)}) collective-permute-start(bf16[32,1536]{1,0:T(8,128)(2,1)S(1)} %shard_map.149.own_ref), channel_id=1, source_target_pairs={{0,8},{4,12},{8,0},{12,4},{1,9},{5,13},{9,1},{13,5},{2,10},{6,14},... | collective-permute-start | bytes 294920 | tf_op jit(solution)/shard_map/ppermute | solution.py:181
  53.9 1.5 %collective-permute-done.10.got_ref = bf16[32,2176]{1,0:T(8,128)(2,1)S(1)} collective-permute-done((bf16[32,2176]{1,0:T(8,128)(2,1)S(1)}, bf16[32,2176]{1,0:T(8,128)(2,1)S(1)}, u32[]{:S(2)}, u32[]{:S(2)}) %collective-permute-start.10) | collective-permute-done | bytes 139296 | tf_op jit(solution)/shard_map/ppermute | solution.py:181
  55.6 0.8 %shard_map.151.refs_0_ = f32[32,2048]{1,0:T(8,128)S(1)} custom-call(bf16[32,1024]{1,0:T(8,128)(2,1)S(1)} %get-tuple-element.42.hidden_ref, bf16[3584,2048]{1,0:T(8,128)(2,1)S(1)} %bitcast.4), custom_call_target="tpu_custom_call" | custom-call | flops 1000000000 | bytes 1048576 | tf_op jit(solution)/shard_map/pallas_call | solution.py:191
  56.8 0.8 %shard_map.152._.refs_0_ = f32[32,2048]{1,0:T(8,128)S(1)} custom-call(bf16[32,1024]{1,0:T(8,128)(2,1)S(1)} %collective-permute-done.11.hidden_ref, bf16[3584,2048]{1,0:T(8,128)(2,1)S(1)} %bitcast.4, f32[32,2048]{1,0:T(8,128)S(1)} %shard_map.151.refs_0_), custom_call_target="tpu_custom_call" | custom-call | flops 1000000000 | bytes 1048576 | tf_op jit(solution)/shard_map/pallas_call | solution.py:191
  58.0 0.6 shard_map.154.before_ref
  59.1 0.7 shard_map.155
  59.8 0.9 %collective-permute-start.14 = (bf16[8,2048]{1,0:T(8,128)(2,1)S(1)}, bf16[8,2048]{1,0:T(8,128)(2,1)S(1)}, u32[]{:S(2)}, u32[]{:S(2)}) collective-permute-start(bf16[8,2048]{1,0:T(8,128)(2,1)S(1)} %get-tuple-element.45), channel_id=1, source_target_pairs={{0,2},{1,3},{2,0},{3,1},{4,6},{5,7},{6,4},{7,5},{8,10},{9,11},{10,... | collective-permute-start | bytes 98312 | tf_op jit(solution)/shard_map/ppermute | solution.py:181
  60.7 3.5 %collective-permute-start.15 = (bf16[8,2048]{1,0:T(8,128)(2,1)S(1)}, bf16[8,2048]{1,0:T(8,128)(2,1)S(1)}, u32[]{:S(2)}, u32[]{:S(2)}) collective-permute-start(bf16[8,2048]{1,0:T(8,128)(2,1)S(1)} %get-tuple-element.46), channel_id=1, source_target_pairs={{0,3},{1,2},{2,1},{3,0},{4,7},{5,6},{6,5},{7,4},{8,11},{9,10},{10,... | collective-permute-start | bytes 98312 | tf_op jit(solution)/shard_map/ppermute | solution.py:181
  64.7 1.7 %collective-permute-done.15 = bf16[8,2048]{1,0:T(8,128)(2,1)S(1)} collective-permute-done((bf16[8,2048]{1,0:T(8,128)(2,1)S(1)}, bf16[8,2048]{1,0:T(8,128)(2,1)S(1)}, u32[]{:S(2)}, u32[]{:S(2)}) %collective-permute-start.15) | collective-permute-done | bytes 32800 | tf_op jit(solution)/shard_map/ppermute | solution.py:181
  66.4 0.7 %add_convert_fusion = bf16[8,2048]{1,0:T(8,128)(2,1)} fusion(bf16[8,2048]{1,0:T(8,128)(2,1)S(1)} %collective-permute-done.15, bf16[8,2048]{1,0:T(8,128)(2,1)S(1)} %collective-permute-done.14, bf16[8,2048]{1,0:T(8,128)(2,1)S(1)} %collective-permute-done.13, bf16[8,2048]{1,0:T(8,128)(2,1)S(1)} %get-tuple-element.43, bf16[8,1024]{1,0:T(8,128)(2,1)S(1)} %get-tuple-element.36, ...), kind=kLoop, calls=%fused_computation | loop fusion | flops 229376 | bytes 196640 | tf_op jit(solution)/shard_map/convert_element_type | solution.py:712
  (59 shorter events, 3.3 us)
Async XLA Ops:
  0.0 11.7 %copy-start.6 = (bf16[8,2048]{1,0:T(8,128)(2,1)S(1)}, bf16[8,2048]{1,0:T(8,128)(2,1)}, u32[]{:S(2)}) copy-start(bf16[8,2048]{1,0:T(8,128)(2,1)} %refs_0_.1) | copy-start | bytes 98308
  0.0 11.7 %copy-start.5 = (bf16[2048,128]{1,0:T(8,128)(2,1)S(1)}, bf16[2048,128]{1,0:T(8,128)(2,1)}, u32[]{:S(2)}) copy-start(bf16[2048,128]{1,0:T(8,128)(2,1)} %refs_7_.1) | copy-start | bytes 1572868
  0.0 11.7 %copy-start.4 = (bf16[2048,128]{1,0:T(8,128)(2,1)S(1)}, bf16[2048,128]{1,0:T(8,128)(2,1)}, u32[]{:S(2)}) copy-start(bf16[2048,128]{1,0:T(8,128)(2,1)} %refs_6_.3) | copy-start | bytes 1572868
  0.0 11.7 %copy-start.3 = (bf16[2048,1024]{1,0:T(8,128)(2,1)S(1)}, bf16[2048,1024]{1,0:T(8,128)(2,1)}, u32[]{:S(2)}) copy-start(bf16[2048,1024]{1,0:T(8,128)(2,1)} %refs_5_.3) | copy-start | bytes 12582916
  0.0 11.7 %copy-start.7 = (f32[2048]{0:T(1024)S(1)}, f32[2048]{0:T(1024)}, u32[]{:S(2)}) copy-start(f32[2048]{0:T(1024)} %param.15) | copy-start | bytes 24580
  0.0 22.7 %copy-start.9 = (bf16[2,256,512]{2,1,0:T(8,128)(2,1)S(1)}, bf16[2,256,512]{2,1,0:T(8,128)(2,1)}, u32[]{:S(2)}) copy-start(bf16[2,256,512]{2,1,0:T(8,128)(2,1)} %values_ref.1) | copy-start | bytes 1572868
  0.0 22.7 %copy-start.8 = (bf16[2,256,512]{2,1,0:T(8,128)(2,1)S(1)}, bf16[2,256,512]{2,1,0:T(8,128)(2,1)}, u32[]{:S(2)}) copy-start(bf16[2,256,512]{2,1,0:T(8,128)(2,1)} %keys_ref.1) | copy-start | bytes 1572868
  0.0 33.1 %copy-start = (bf16[1024,2048]{1,0:T(8,128)(2,1)S(1)}, bf16[1024,2048]{1,0:T(8,128)(2,1)}, u32[]{:S(2)}) copy-start(bf16[1024,2048]{1,0:T(8,128)(2,1)} %w_ref.7) | copy-start | bytes 12582916
  0.0 7.0 %collective-permute-start.1 = (bf16[8,2048]{1,0:T(8,128)(2,1)}, bf16[8,2048]{1,0:T(8,128)(2,1)S(1)}, u32[]{:S(2)}, u32[]{:S(2)}) collective-permute-start(bf16[8,2048]{1,0:T(8,128)(2,1)} %refs_0_.1), channel_id=1, source_target_pairs={{0,2},{1,3},{2,0},{3,1},{4,6},{5,7},{6,4},{7,5},{8,10},{9,11},{10,... | collective-permute-start | bytes 98312 | tf_op jit(solution)/shard_map/ppermute | solution.py:181
  4.2 4.1 %collective-permute-start = (bf16[8,2048]{1,0:T(8,128)(2,1)}, bf16[8,2048]{1,0:T(8,128)(2,1)S(1)}, u32[]{:S(2)}, u32[]{:S(2)}) collective-permute-start(bf16[8,2048]{1,0:T(8,128)(2,1)} %refs_0_.1), channel_id=1, source_target_pairs={{0,1},{1,0},{2,3},{3,2},{4,5},{5,4},{6,7},{7,6},{8,9},{9,8},{10,11... | collective-permute-start | bytes 98312 | tf_op jit(solution)/shard_map/ppermute | solution.py:181
  5.8 5.9 %collective-permute-start.2 = (bf16[8,2048]{1,0:T(8,128)(2,1)}, bf16[8,2048]{1,0:T(8,128)(2,1)S(1)}, u32[]{:S(2)}, u32[]{:S(2)}) collective-permute-start(bf16[8,2048]{1,0:T(8,128)(2,1)} %refs_0_.1), channel_id=1, source_target_pairs={{0,3},{1,2},{2,1},{3,0},{4,7},{5,6},{6,5},{7,4},{8,11},{9,10},{10,... | collective-permute-start | bytes 98312 | tf_op jit(solution)/shard_map/ppermute | solution.py:181
  6.4 39.1 %copy-start.2 = (bf16[2048,3584]{1,0:T(8,128)(2,1)S(1)}, bf16[2048,3584]{1,0:T(8,128)(2,1)}, u32[]{:S(2)}) copy-start(bf16[2048,3584]{1,0:T(8,128)(2,1)} %wu_ref.5) | copy-start | bytes 44040196
  7.0 38.5 %copy-start.1 = (bf16[2048,3584]{1,0:T(8,128)(2,1)S(1)}, bf16[2048,3584]{1,0:T(8,128)(2,1)}, u32[]{:S(2)}) copy-start(bf16[2048,3584]{1,0:T(8,128)(2,1)} %wg_ref.5) | copy-start | bytes 44040196
  7.0 38.5 %copy-start.10 = (f32[2048]{0:T(1024)S(1)}, f32[2048]{0:T(1024)}, u32[]{:S(2)}) copy-start(f32[2048]{0:T(1024)} %param.24) | copy-start | bytes 24580
  7.0 38.5 %copy-start.12 = (s32[32]{0:T(128)S(1)}, s32[32]{0:T(128)}, u32[]{:S(2)}) copy-start(s32[32]{0:T(128)} %param.23) | copy-start | bytes 388
  33.6 4.8 %collective-permute-start.3 = (bf16[32,1024]{1,0:T(8,128)(2,1)S(1)}, bf16[32,1024]{1,0:T(8,128)(2,1)S(1)}, u32[]{:S(2)}, u32[]{:S(2)}) collective-permute-start(bf16[32,1024]{1,0:T(8,128)(2,1)S(1)} %get-tuple-element.30.keep_ref), channel_id=1, source_target_pairs={{0,1},{1,0},{2,3},{3,2},{4,5},{5,4},{6,7},{7,6},{8,9},{9,8},{10,11... | collective-permute-start | bytes 196616 | tf_op jit(solution)/shard_map/ppermute | solution.py:181
  34.4 4.8 %collective-permute-start.5 = (bf16[32,1024]{1,0:T(8,128)(2,1)S(1)}, bf16[32,1024]{1,0:T(8,128)(2,1)S(1)}, u32[]{:S(2)}, u32[]{:S(2)}) collective-permute-start(bf16[32,1024]{1,0:T(8,128)(2,1)S(1)} %shard_map.142.keep_ref), channel_id=1, source_target_pairs={{0,1},{1,0},{2,3},{3,2},{4,5},{5,4},{6,7},{7,6},{8,9},{9,8},{10,11... | collective-permute-start | bytes 196616 | tf_op jit(solution)/shard_map/ppermute | solution.py:181
  38.5 7.0 %collective-permute-start.4 = (bf16[32,1024]{1,0:T(8,128)(2,1)S(1)}, bf16[32,1024]{1,0:T(8,128)(2,1)S(1)}, u32[]{:S(2)}, u32[]{:S(2)}) collective-permute-start(bf16[32,1024]{1,0:T(8,128)(2,1)S(1)} %shard_map.140.refs_2_), channel_id=1, source_target_pairs={{0,2},{1,3},{2,0},{3,1},{4,6},{5,7},{6,4},{7,5},{8,10},{9,11},{10,... | collective-permute-start | bytes 196616 | tf_op jit(solution)/shard_map/ppermute | solution.py:181
  39.3 7.1 %collective-permute-start.6 = (bf16[32,1024]{1,0:T(8,128)(2,1)S(1)}, bf16[32,1024]{1,0:T(8,128)(2,1)S(1)}, u32[]{:S(2)}, u32[]{:S(2)}) collective-permute-start(bf16[32,1024]{1,0:T(8,128)(2,1)S(1)} %shard_map.143.refs_2_), channel_id=1, source_target_pairs={{0,2},{1,3},{2,0},{3,1},{4,6},{5,7},{6,4},{7,5},{8,10},{9,11},{10,... | collective-permute-start | bytes 196616 | tf_op jit(solution)/shard_map/ppermute | solution.py:181
  47.3 1.6 %collective-permute-start.7 = (bf16[32,2176]{1,0:T(8,128)(2,1)S(1)}, bf16[32,2176]{1,0:T(8,128)(2,1)S(1)}, u32[]{:S(2)}, u32[]{:S(2)}) collective-permute-start(bf16[32,2176]{1,0:T(8,128)(2,1)S(1)} %get-tuple-element.40), channel_id=1, source_target_pairs={{0,4},{4,0},{8,12},{12,8},{1,5},{5,1},{9,13},{13,9},{2,6},{6,2},{1... | collective-permute-start | bytes 417800 | tf_op jit(solution)/shard_map/ppermute | solution.py:181
  49.1 6.3 %collective-permute-start.10 = (bf16[32,2176]{1,0:T(8,128)(2,1)S(1)}, bf16[32,2176]{1,0:T(8,128)(2,1)S(1)}, u32[]{:S(2)}, u32[]{:S(2)}) collective-permute-start(bf16[32,2176]{1,0:T(8,128)(2,1)S(1)} %shard_map.147.refs_0_.own_ref), channel_id=1, source_target_pairs={{0,8},{4,12},{8,0},{12,4},{1,9},{5,13},{9,1},{13,5},{2,10},{6,14},... | collective-permute-start | bytes 417800 | tf_op jit(solution)/shard_map/ppermute | solution.py:181
  49.3 6.2 %slice-start = ((s8[14680064]{0:T(1024)(128)(4,1)}), s8[2097152]{0:T(1024)(128)(4,1)S(1)}, s32[]{:S(2)}) async-start(s8[14680064]{0:T(1024)(128)(4,1)} %bitcast.3), calls=%async_computation.2 | async-start | bytes 4194304
  49.3 6.2 %slice-start.1 = ((s8[14680064]{0:T(1024)(128)(4,1)}), s8[4194304]{0:T(1024)(128)(4,1)S(1)}, s32[]{:S(2)}) async-start(s8[14680064]{0:T(1024)(128)(4,1)} %bitcast.3), calls=%async_computation.3 | async-start | bytes 8388608
  49.3 6.3 %slice-start.2 = ((s8[14680064]{0:T(1024)(128)(4,1)}), s8[4194304]{0:T(1024)(128)(4,1)S(1)}, s32[]{:S(2)}) async-start(s8[14680064]{0:T(1024)(128)(4,1)} %bitcast.3), calls=%async_computation.4 | async-start | bytes 8388608
  50.5 5.1 %slice-start.3 = ((s8[14680064]{0:T(1024)(128)(4,1)}), s8[4194304]{0:T(1024)(128)(4,1)S(1)}, s32[]{:S(2)}) async-start(s8[14680064]{0:T(1024)(128)(4,1)} %bitcast.3), calls=%async_computation.5 | async-start | bytes 8388608
  50.5 1.5 %collective-permute-start.8 = (bf16[32,1536]{1,0:T(8,128)(2,1)S(1)}, bf16[32,1536]{1,0:T(8,128)(2,1)S(1)}, u32[]{:S(2)}, u32[]{:S(2)}) collective-permute-start(bf16[32,1536]{1,0:T(8,128)(2,1)S(1)} %shard_map.148), channel_id=1, source_target_pairs={{0,4},{4,0},{8,12},{12,8},{1,5},{5,1},{9,13},{13,9},{2,6},{6,2},{1... | collective-permute-start | bytes 294920 | tf_op jit(solution)/shard_map/ppermute | solution.py:181
  52.1 5.6 %collective-permute-start.9 = (bf16[32,1536]{1,0:T(8,128)(2,1)S(1)}, bf16[32,1536]{1,0:T(8,128)(2,1)S(1)}, u32[]{:S(2)}, u32[]{:S(2)}) collective-permute-start(bf16[32,1536]{1,0:T(8,128)(2,1)S(1)} %shard_map.149.own_ref), channel_id=1, source_target_pairs={{0,8},{4,12},{8,0},{12,4},{1,9},{5,13},{9,1},{13,5},{2,10},{6,14},... | collective-permute-start | bytes 294920 | tf_op jit(solution)/shard_map/ppermute | solution.py:181
  55.5 1.3 %collective-permute-start.11 = (bf16[32,1024]{1,0:T(8,128)(2,1)S(1)}, bf16[32,1024]{1,0:T(8,128)(2,1)S(1)}, u32[]{:S(2)}, u32[]{:S(2)}) collective-permute-start(bf16[32,1024]{1,0:T(8,128)(2,1)S(1)} %get-tuple-element.42.hidden_ref), channel_id=1, source_target_pairs={{0,4},{4,0},{8,12},{12,8},{1,5},{5,1},{9,13},{13,9},{2,6},{6,2},{1... | collective-permute-start | bytes 196616 | tf_op jit(solution)/shard_map/ppermute | solution.py:181
  57.8 1.3 %collective-permute-start.12 = (bf16[32,768]{1,0:T(8,128)(2,1)S(1)}, bf16[32,768]{1,0:T(8,128)(2,1)S(1)}, u32[]{:S(2)}, u32[]{:S(2)}) collective-permute-start(bf16[32,768]{1,0:T(8,128)(2,1)S(1)} %shard_map.153.hidden_ref), channel_id=1, source_target_pairs={{0,4},{4,0},{8,12},{12,8},{1,5},{5,1},{9,13},{13,9},{2,6},{6,2},{1... | collective-permute-start | bytes 147464 | tf_op jit(solution)/shard_map/ppermute | solution.py:181
  59.7 4.6 %collective-permute-start.13 = (bf16[8,2048]{1,0:T(8,128)(2,1)S(1)}, bf16[8,2048]{1,0:T(8,128)(2,1)S(1)}, u32[]{:S(2)}, u32[]{:S(2)}) collective-permute-start(bf16[8,2048]{1,0:T(8,128)(2,1)S(1)} %get-tuple-element.44), channel_id=1, source_target_pairs={{0,1},{1,0},{2,3},{3,2},{4,5},{5,4},{6,7},{7,6},{8,9},{9,8},{10,11... | collective-permute-start | bytes 98312 | tf_op jit(solution)/shard_map/ppermute | solution.py:181
  59.8 4.9 %collective-permute-start.14 = (bf16[8,2048]{1,0:T(8,128)(2,1)S(1)}, bf16[8,2048]{1,0:T(8,128)(2,1)S(1)}, u32[]{:S(2)}, u32[]{:S(2)}) collective-permute-start(bf16[8,2048]{1,0:T(8,128)(2,1)S(1)} %get-tuple-element.45), channel_id=1, source_target_pairs={{0,2},{1,3},{2,0},{3,1},{4,6},{5,7},{6,4},{7,5},{8,10},{9,11},{10,... | collective-permute-start | bytes 98312 | tf_op jit(solution)/shard_map/ppermute | solution.py:181
  60.7 5.7 %collective-permute-start.15 = (bf16[8,2048]{1,0:T(8,128)(2,1)S(1)}, bf16[8,2048]{1,0:T(8,128)(2,1)S(1)}, u32[]{:S(2)}, u32[]{:S(2)}) collective-permute-start(bf16[8,2048]{1,0:T(8,128)(2,1)S(1)} %get-tuple-element.46), channel_id=1, source_target_pairs={{0,3},{1,2},{2,1},{3,0},{4,7},{5,6},{6,5},{7,4},{8,11},{9,10},{10,... | collective-permute-start | bytes 98312 | tf_op jit(solution)/shard_map/ppermute | solution.py:181
  (1 other events, 0.7 us)
